TPU v7x, 256 devices: a whole 4x4x8 slice. The times are simulated.
256 devices in a mesh: fsdp: 16 (over y, x), ep: 16 (over z, core).
Axes of the slice: x: 4, y: 4, z: 8, core: 2. Of those that a mesh axis runs over, the one named last changes fastest.
Arguments:
- tokens: bfloat16 [8192, 7168], P('ep', 'fsdp'), may hold values from -6 to 6
- cotangent: bfloat16 [8192, 7168], P('ep', 'fsdp'), may hold values from -3 to 3
- gate_weight: bfloat16 [16, 7168, 2048], P('ep', None, 'fsdp'), may hold values from -0.0625 to 0.0625
- up_weight: bfloat16 [16, 7168, 2048], P('ep', None, 'fsdp'), may hold values from -0.0625 to 0.0625
- down_weight: bfloat16 [16, 2048, 7168], P('ep', 'fsdp'), may hold values from -0.125 to 0.125
- chosen: int32 [16, 16, 16], P(None, 'ep'), may hold values from 0 to 511, as said below
- counts: int32 [16, 16], P(None, 'ep'), may hold values from 1 to 16, as said below
- gate_prob: float32 [16, 16, 16], P(None, 'ep'), may hold values from 0.2 to 1
Outputs:
- mixture: bfloat16 [8192, 7168], P('ep', 'fsdp')
- grad_tokens: bfloat16 [8192, 7168], P('ep', 'fsdp')
- grad_gate: bfloat16 [16, 7168, 2048], P('ep', None, 'fsdp')
- grad_up: bfloat16 [16, 7168, 2048], P('ep', None, 'fsdp')
- grad_down: bfloat16 [16, 2048, 7168], P('ep', 'fsdp')
Inputs may be any that keep to these rules, and one draw needn't show every extreme that they name: For each expert e and group s the entries chosen[e, s, j] with j < counts[e, s] are distinct; the remaining entries are padding. `counts`: in every draw one expert takes 16 rows from every group.
All inputs are finite; a program needn't handle non-finite values.
Results may differ from a plain program's by a relative error of at most 0.017.
Values may be sent and summed in bfloat16 or wider, within the bound.
A program may use at most 192 MiB of HBM per device.

v0:
```python
import jax
import jax.numpy as jnp
from jax import lax
from jax.sharding import PartitionSpec as P


def pick_rows(tokens, cotangent, row_index, live_mask, weight):
    flat_rows = row_index.reshape(-1)
    keep_rows = live_mask.reshape(-1)[:, None]
    taken_tokens = jnp.take(tokens, flat_rows, axis=0)
    picked_tokens = jnp.where(keep_rows, taken_tokens, jnp.zeros_like(taken_tokens))
    taken_grads = jnp.take(cotangent, flat_rows, axis=0).astype(jnp.float32)
    picked_grads = (weight.reshape(-1)[:, None] * taken_grads).astype(jnp.bfloat16)
    shaped = row_index.shape + (tokens.shape[1],)
    return (picked_tokens.reshape(shaped), picked_grads.reshape(shaped))


def to_slots(summed, experts, slot_count):
    return summed.astype(jnp.bfloat16).reshape(experts, slot_count, summed.shape[1])


def send_back(term, experts, slot_count):
    summed = lax.psum_scatter(
        term.astype(jnp.bfloat16), "fsdp", scatter_dimension=1, tiled=True
    ).astype(jnp.float32)
    return lax.all_to_all(
        to_slots(summed, experts, slot_count), "ep", split_axis=0, concat_axis=0, tiled=True
    )


def per_device(tokens, cotangent, gate_weight, up_weight, down_weight, chosen, counts, gate_prob):
    experts = chosen.shape[0]
    slot_count = chosen.shape[2]
    features = tokens.shape[1]
    row_index = chosen[:, 0, :]
    position = lax.broadcasted_iota(jnp.int32, (experts, slot_count), 1)
    live_mask = position < counts
    weight = jnp.where(live_mask, gate_prob[:, 0, :], 0.0)
    picked_tokens, picked_grads = pick_rows(tokens, cotangent, row_index, live_mask, weight)
    wide_tokens, wide_grads = (
        lax.all_gather(picked_tokens, "fsdp", axis=2, tiled=True),
        lax.all_gather(picked_grads, "fsdp", axis=2, tiled=True),
    )
    rows_tokens, rows_grads = (
        lax.all_to_all(wide_tokens, "ep", split_axis=0, concat_axis=0, tiled=True),
        lax.all_to_all(wide_grads, "ep", split_axis=0, concat_axis=0, tiled=True),
    )
    full_width = rows_tokens.shape[2]
    total_rows = rows_tokens.shape[0] * slot_count
    rows_tokens = rows_tokens.reshape(total_rows, full_width)
    rows_grads = rows_grads.reshape(total_rows, full_width)
    gate_local = gate_weight[0]
    up_local = up_weight[0]
    down_local = down_weight[0]
    pre_gate = jnp.dot(rows_tokens, gate_local, preferred_element_type=jnp.float32)
    pre_up = jnp.dot(rows_tokens, up_local, preferred_element_type=jnp.float32)
    sigmoid_gate = jax.nn.sigmoid(pre_gate)
    activated = pre_gate * sigmoid_gate
    hidden = (activated * pre_up).astype(jnp.bfloat16)
    output_term = jnp.dot(hidden, down_local, preferred_element_type=jnp.float32)
    output_back = send_back(output_term, experts, slot_count)
    contract_rows = (((0,), (0,)), ((), ()))
    contract_last = (((1,), (1,)), ((), ()))
    grad_hidden = lax.dot_general(
        rows_grads, down_local, contract_last, preferred_element_type=jnp.float32
    )
    grad_pre_gate = (
        grad_hidden * pre_up * sigmoid_gate * (1.0 + pre_gate * (1.0 - sigmoid_gate))
    ).astype(jnp.bfloat16)
    grad_pre_up = (grad_hidden * activated).astype(jnp.bfloat16)
    grad_down = lax.dot_general(
        hidden, rows_grads, contract_rows, preferred_element_type=jnp.float32
    ).astype(jnp.bfloat16)
    grad_gate = lax.dot_general(
        rows_tokens, grad_pre_gate, contract_rows, preferred_element_type=jnp.float32
    ).astype(jnp.bfloat16)
    grad_up = lax.dot_general(
        rows_tokens, grad_pre_up, contract_rows, preferred_element_type=jnp.float32
    ).astype(jnp.bfloat16)
    grad_term = lax.dot_general(
        grad_pre_gate, gate_local, contract_last, preferred_element_type=jnp.float32
    )
    grad_term = grad_term + lax.dot_general(
        grad_pre_up, up_local, contract_last, preferred_element_type=jnp.float32
    )
    grad_back = send_back(grad_term, experts, slot_count)
    flat_rows = row_index.reshape(-1)
    output_rows = output_back.reshape(-1, features).astype(jnp.float32)
    mixture = (
        jnp.zeros((tokens.shape[0], features), jnp.float32)
        .at[flat_rows]
        .add(weight.reshape(-1)[:, None] * output_rows)
    )
    grad_rows = jnp.where(
        live_mask.reshape(-1)[:, None], grad_back.reshape(-1, features).astype(jnp.float32), 0.0
    )
    grad_tokens = jnp.zeros((tokens.shape[0], features), jnp.float32).at[flat_rows].add(grad_rows)
    return (
        mixture.astype(jnp.bfloat16),
        grad_tokens.astype(jnp.bfloat16),
        grad_gate[None],
        grad_up[None],
        grad_down[None],
    )


def solution(mesh):
    placed = (
        P("ep", "fsdp"),
        P("ep", "fsdp"),
        P("ep", None, "fsdp"),
        P("ep", None, "fsdp"),
        P("ep", "fsdp", None),
        P(None, "ep", None),
        P(None, "ep"),
        P(None, "ep", None),
    )
    return jax.shard_map(
        per_device,
        mesh=mesh,
        in_specs=placed,
        out_specs=(
            P("ep", "fsdp"),
            P("ep", "fsdp"),
            P("ep", None, "fsdp"),
            P("ep", None, "fsdp"),
            P("ep", "fsdp", None),
        ),
        check_vma=False,
    )
```

profile of v0, /device:TPU:1, one launch (start us, length us, event | category | flops | bytes accessed | tf_op | source)
XLA Modules:
  0.0 701.6 jit_solution(7673215205043818833)
XLA Ops:
  11.5 1.9 copy.32
  16.3 1.9 copy.36
  18.3 179.5 %all-gather.3.cloned.1.call-done = bf16[16,16,7168]{1,0,2:T(8,128)(2,1)} async-done(((bf16[16,16,448]{1,0,2:T(8,128)(2,1)}), bf16[16,16,7168]{1,0,2:T(8,128)(2,1)}) %all-gather.3.cloned.1.call-update) | async-done | bytes 3670032 | tf_op jit(solution)/shard_map/all_gather | solution.py:41
  197.8 26.9 %copy.33 = bf16[16,16,7168]{2,1,0:T(8,128)(2,1)} copy(bf16[16,16,7168]{1,0,2:T(8,128)(2,1)} %all-gather.3.cloned.1.call-done) | data formatting | bytes 7340032 | tf_op jit(solution)/shard_map/all_gather | solution.py:41
  224.7 7.9 %all-to-all-start = ((bf16[16,16,7168]{2,1,0:T(8,128)(2,1)}), bf16[16,16,7168]{2,1,0:T(8,128)(2,1)}, u32[]{:S(2)}, u32[]{:S(2)}) async-start(bf16[16,16,7168]{2,1,0:T(8,128)(2,1)} %copy.33), calls=%async_computation | async-start | bytes 7340032 | tf_op jit(solution)/shard_map/all_to_all | solution.py:45
  232.6 148.5 %all-gather.5.cloned.1.call-done = bf16[16,16,7168]{1,0,2:T(8,128)(2,1)} async-done(((bf16[16,16,448]{1,0,2:T(8,128)(2,1)}), bf16[16,16,7168]{1,0,2:T(8,128)(2,1)}) %all-gather.5.cloned.1.call-update) | async-done | bytes 3670032 | tf_op jit(solution)/shard_map/all_gather | solution.py:42
  381.1 26.5 %copy.37 = bf16[16,16,7168]{2,1,0:T(8,128)(2,1)} copy(bf16[16,16,7168]{1,0,2:T(8,128)(2,1)} %all-gather.5.cloned.1.call-done) | data formatting | bytes 7340032 | tf_op jit(solution)/shard_map/all_gather | solution.py:42
  407.6 7.9 %all-to-all-start.2 = ((bf16[16,16,7168]{2,1,0:T(8,128)(2,1)}), bf16[16,16,7168]{2,1,0:T(8,128)(2,1)}, u32[]{:S(2)}, u32[]{:S(2)}) async-start(bf16[16,16,7168]{2,1,0:T(8,128)(2,1)} %copy.37), calls=%async_computation.3 | async-start | bytes 7340032 | tf_op jit(solution)/shard_map/all_to_all | solution.py:46
  415.5 3.8 fusion.8
  419.4 3.2 fusion.12
  422.6 75.2 %all-to-all-done.2 = bf16[16,16,7168]{2,1,0:T(8,128)(2,1)} async-done(((bf16[16,16,7168]{2,1,0:T(8,128)(2,1)}), bf16[16,16,7168]{2,1,0:T(8,128)(2,1)}, u32[]{:S(2)}, u32[]{:S(2)}) %all-to-all-start.2) | async-done | bytes 3670048 | tf_op jit(solution)/shard_map/all_to_all | solution.py:46
  497.7 3.2 multiply_convert_fusion.1
  500.9 3.1 convolution_convert_fusion
  504.1 2.7 fusion.10
  506.8 2.9 fusion
  511.2 71.2 %reduce-scatter.3.cloned.1.call-done = bf16[256,448]{0,1:T(8,128)(2,1)} async-done(((bf16[256,7168]{0,1:T(8,128)(2,1)}), bf16[256,448]{0,1:T(8,128)(2,1)}) %reduce-scatter.3.cloned.1.call-update) | async-done | bytes 229392 | tf_op jit(solution)/shard_map/reduce_scatter | solution.py:23
  584.2 9.4 %all-to-all-start.1 = ((bf16[16,16,448]{2,1,0:T(8,128)(2,1)}), bf16[16,16,448]{2,1,0:T(8,128)(2,1)S(1)}, u32[]{:S(2)}, u32[]{:S(2)}) async-start(bf16[16,16,448]{2,1,0:T(8,128)(2,1)} %bitcast.7), calls=%async_computation.2 | async-start | bytes 524288 | tf_op jit(solution)/shard_map/all_to_all | solution.py:26
  593.6 3.9 fusion.3
  597.5 70.1 %reduce-scatter.5.cloned.1.call-done = bf16[256,448]{0,1:T(8,128)(2,1)} async-done(((bf16[256,7168]{0,1:T(8,128)(2,1)}), bf16[256,448]{0,1:T(8,128)(2,1)}) %reduce-scatter.5.cloned.1.call-update) | async-done | bytes 229392 | tf_op jit(solution)/shard_map/reduce_scatter | solution.py:23
  669.4 9.4 %all-to-all-start.3 = ((bf16[16,16,448]{2,1,0:T(8,128)(2,1)}), bf16[16,16,448]{2,1,0:T(8,128)(2,1)}, u32[]{:S(2)}, u32[]{:S(2)}) async-start(bf16[16,16,448]{2,1,0:T(8,128)(2,1)} %bitcast.11), calls=%async_computation.5 | async-start | bytes 524288 | tf_op jit(solution)/shard_map/all_to_all | solution.py:26
  678.8 4.4 fusion.2
  683.2 4.4 fusion.1
  687.6 2.4 scatter_custom_fusion
  691.1 2.8 scatter_custom_fusion.1
  (49 shorter events, 14.3 us)
Async XLA Ops:
  7.2 490.6 %copy-start = (bf16[1,128,7168]{2,1,0:T(8,128)(2,1)S(1)}, bf16[1,128,7168]{2,1,0:T(8,128)(2,1)}, u32[]{:S(2)}) copy-start(bf16[1,128,7168]{2,1,0:T(8,128)(2,1)} %param.14) | copy-start | bytes 5505028
  7.2 190.6 %all-gather.3.cloned.1.call-start = ((), (), s32[]{:S(2)}) async-start(), calls=%async_computation.6 | async-start | bytes 31195136 | tf_op jit(solution)/shard_map/all_gather | solution.py:41
  9.0 5.1 copy-start.5
  10.2 4.6 copy-start.3
  13.5 367.6 %all-gather.5.cloned.1.call-start = ((), (), s32[]{:S(2)}) async-start(), calls=%async_computation.8 | async-start | bytes 31195136 | tf_op jit(solution)/shard_map/all_gather | solution.py:42
  224.7 182.9 %all-to-all-start = ((bf16[16,16,7168]{2,1,0:T(8,128)(2,1)}), bf16[16,16,7168]{2,1,0:T(8,128)(2,1)}, u32[]{:S(2)}, u32[]{:S(2)}) async-start(bf16[16,16,7168]{2,1,0:T(8,128)(2,1)} %copy.33), calls=%async_computation | async-start | bytes 7340032 | tf_op jit(solution)/shard_map/all_to_all | solution.py:45
  407.6 90.1 %all-to-all-start.2 = ((bf16[16,16,7168]{2,1,0:T(8,128)(2,1)}), bf16[16,16,7168]{2,1,0:T(8,128)(2,1)}, u32[]{:S(2)}, u32[]{:S(2)}) async-start(bf16[16,16,7168]{2,1,0:T(8,128)(2,1)} %copy.37), calls=%async_computation.3 | async-start | bytes 7340032 | tf_op jit(solution)/shard_map/all_to_all | solution.py:46
  415.5 166.9 %reduce-scatter.3.cloned.1.call-start = ((), (), s32[]{:S(2)}) async-start(), calls=%async_computation.7 | async-start | bytes 3899392 | tf_op jit(solution)/shard_map/reduce_scatter | solution.py:23
  415.5 3.9 copy-start.2
  504.0 163.6 %reduce-scatter.5.cloned.1.call-start = ((), (), s32[]{:S(2)}) async-start(), calls=%async_computation.9 | async-start | bytes 3899392 | tf_op jit(solution)/shard_map/reduce_scatter | solution.py:23
  504.1 2.8 copy-start.1
  509.8 0.7 copy-start.4
  584.2 85.2 %all-to-all-start.1 = ((bf16[16,16,448]{2,1,0:T(8,128)(2,1)}), bf16[16,16,448]{2,1,0:T(8,128)(2,1)S(1)}, u32[]{:S(2)}, u32[]{:S(2)}) async-start(bf16[16,16,448]{2,1,0:T(8,128)(2,1)} %bitcast.7), calls=%async_computation.2 | async-start | bytes 524288 | tf_op jit(solution)/shard_map/all_to_all | solution.py:26
  669.4 21.7 %all-to-all-start.3 = ((bf16[16,16,448]{2,1,0:T(8,128)(2,1)}), bf16[16,16,448]{2,1,0:T(8,128)(2,1)}, u32[]{:S(2)}, u32[]{:S(2)}) async-start(bf16[16,16,448]{2,1,0:T(8,128)(2,1)} %bitcast.11), calls=%async_computation.5 | async-start | bytes 524288 | tf_op jit(solution)/shard_map/all_to_all | solution.py:26
Sparse Core Ops, SparseCore 0:
  13.6 184.1 all-gather.2
  200.8 180.2 all-gather.4
  504.1 78.2 reduce-scatter.2
  585.9 81.6 reduce-scatter.4
where the time goes:
time: 704 us; the launch traced here: 702 us
  waiting for transfers between devices  545 us (77%)
  local copies, waits for them, and re-layouts  68.8 us (10%)
  starting transfers between devices  34.7 us (5%)
  matrix products  31.8 us (5%)
  between operations  13.9 us (2%)
  other arithmetic  7.78 us (1%)
    all_gather x1, waiting for transfers between devices, per_device(): lax.all_gather(picked_tokens, 'fsdp', axis=2, tiled=True)  180 us
    all_gather x1, waiting for transfers between devices, per_device(): lax.all_gather(picked_grads, 'fsdp', axis=2, tiled=True)  148 us
    reduce_scatter x2, waiting for transfers between devices, send_back(): lax.psum_scatter(term.astype(jnp.bfloat16), 'fsdp', scatter_dimension=1,...  141 us
    all_to_all x1, waiting for transfers between devices, per_device(): lax.all_to_all(wide_grads, 'ep', split_axis=0, concat_axis=0, tiled=True)  75.2 us
    all_gather x1, local copies, waits for them, and re-layouts, per_device(): lax.all_gather(picked_tokens, 'fsdp', axis=2, tiled=True)  26.9 us
    all_gather x1, local copies, waits for them, and re-layouts, per_device(): lax.all_gather(picked_grads, 'fsdp', axis=2, tiled=True)  26.5 us
    all_to_all x2, starting transfers between devices, send_back(): lax.all_to_all(to_slots(summed, experts, slot_count), 'ep', split_axis=0,...  18.8 us
  transfers between devices with their start and end apart: 8, of which 5 were waited for; matrix products, arithmetic and copies ran while one was open for 13% of the time, Pallas kernels for 0%

commit v1 on v0

v1 whole, which is shorter than its diff:
```python
import jax
import jax.numpy as jnp
from jax import lax
from jax.experimental import pallas as pl
from jax.experimental.pallas import tpu as pltpu
from jax.sharding import PartitionSpec as P

MESH = pl.DeviceIdType.MESH
BF = jnp.bfloat16
F32 = jnp.float32
SIDE = 4
RING = (0, -1, 1, 2)
LAST = (((1,), (1,)), ((), ()))
ROWS = (((0,), (0,)), ((), ()))


def dot(a, b, dims=(((1,), (0,)), ((), ()))):
    return lax.dot_general(a, b, dims, preferred_element_type=F32)


def kernel(
    idx_ref, row_idx_ref, w_ref, tok_ref, cot_ref, gate_hbm, up_hbm, down_hbm,
    mixture_ref, grad_tok_ref, ggate_hbm, gup_hbm, gdown_hbm,
    tok_loc, grad_loc, tok_all, grad_all, tok_rem, grad_rem,
    gate, up, down, ggate, gup, gdown,
    out_part, out_rem, ret_part, pre, gh, hid, gpre,
    out_in, out_in2, ret_in, ret_in2, out_res, ret_res, out_back, ret_back,
    w_sem, a2a_send, a2a_recv, ag_send, ag_recv, rs_send, rs_recv, back_send, back_recv, gout_sem,
):
    f = lax.axis_index("fsdp")
    me = lax.axis_index("ep")
    n_ep = idx_ref.shape[0] // 16
    y = lax.div(f, SIDE)
    x = lax.rem(f, SIDE)
    odd = lax.rem(x, 2)
    wide = tok_all.shape[2]
    main = grad_all.shape[2]
    rows = tok_all.shape[1]
    half = rows // 2
    quarter = rows // 4
    feats = tok_ref.shape[1]
    pair = 2 * feats
    slot = 16

    def flat(dy, dx):
        return lax.rem(y + dy + SIDE, SIDE) * SIDE + lax.rem(x + dx + SIDE, SIDE)

    def coord(axis, along, other=0):
        return (other, along) if axis == 0 else (along, other)

    barrier = pltpu.get_barrier_semaphore()
    for dy, dx in ((0, 1), (0, -1), (1, 0), (-1, 0)):
        pl.semaphore_signal(barrier, inc=1, device_id={"fsdp": flat(dy, dx)}, device_id_type=MESH)

    @pl.loop(1, n_ep)
    def _(k):
        pl.semaphore_signal(barrier, inc=1, device_id={"ep": lax.rem(me + k, n_ep)}, device_id_type=MESH)

    loads = [
        pltpu.make_async_copy(src, dst, w_sem.at[i])
        for i, (src, dst) in enumerate(((gate_hbm, gate), (up_hbm, up), (down_hbm, down)))
    ]
    for load in loads:
        load.start()

    n_tok = tok_ref.shape[0]
    fi = lax.broadcasted_iota(jnp.int32, (feats, wide), 0)
    fj = lax.broadcasted_iota(jnp.int32, (feats, wide), 1)

    def packing(delta, low):
        body = (fi == fj + 64 * odd) & (fj < main)
        tail = (fi == fj - delta) & (fj >= low) & (fj < low + 64)
        return jnp.where(body | tail, 1.0, 0.0).astype(BF)

    pack_a = packing(448 * odd, 384 + 64 * odd)
    pack_b = packing(64 + 320 * odd, 448 - 64 * odd)
    hit = lax.broadcasted_iota(jnp.int32, (rows, n_tok), 1) == idx_ref[...]
    onehot = jnp.where(hit, 1.0, 0.0).astype(BF)
    tp = dot(dot(onehot, tok_ref[...]).astype(BF), pack_a)
    gp = dot((dot(onehot, cot_ref[...]) * w_ref[...]).astype(BF), pack_b)
    tok_loc[:, :main] = tp[:, :main].astype(BF)
    tok_loc[:, main:] = (tp[:, main:] + gp[:, main:]).astype(BF)
    grad_loc[...] = gp[:, :main].astype(BF)

    pl.semaphore_wait(barrier, n_ep + 3)

    def scatter(src, dst_of, send, recv):
        @pl.loop(1, n_ep)
        def _(k):
            peer = lax.rem(me + k, n_ep)
            pltpu.make_async_remote_copy(
                src_ref=src.at[pl.ds(peer * slot, slot)],
                dst_ref=dst_of(me * slot),
                send_sem=send,
                recv_sem=recv,
                device_id={"ep": peer},
                device_id_type=MESH,
            ).start()

        pltpu.make_async_copy(src.at[pl.ds(me * slot, slot)], dst_of(me * slot), recv).start()

    def wait_bytes(ref, sem):
        pltpu.make_async_copy(ref, ref, sem).wait()

    part = lax.div(me, n_ep // 2)
    scatter(tok_loc, lambda r: tok_all.at[f, pl.ds(r, slot)], a2a_send.at[0], a2a_recv.at[part])
    scatter(grad_loc, lambda r: grad_all.at[f, pl.ds(r, slot)], a2a_send.at[1], a2a_recv.at[2 + part])

    def put(src, dst, send, recv, axis, step):
        dy, dx = coord(axis, step)
        pltpu.make_async_remote_copy(
            src_ref=src, dst_ref=dst, send_sem=send, recv_sem=recv,
            device_id={"fsdp": flat(dy, dx)}, device_id_type=MESH,
        ).start()

    def gather(buf, which):
        send = ag_send.at[which]

        def sem(h, i):
            return ag_recv.at[which * 40 + h * 20 + i]

        def ref(h, fst, snd, q=None):
            o = coord(h, fst, snd)
            first = h * half + (0 if q is None else q * quarter)
            return buf.at[flat(*o), pl.ds(first, half if q is None else quarter)]

        def wait(h, i, fst, snd, q=None):
            wait_bytes(ref(h, fst, snd, q), sem(h, i))

        def send_block(h, i, fst, snd, axis, step, q=None):
            r = ref(h, fst, snd, q)
            put(r, r, send, sem(h, i), axis, step)

        def own(h):
            for i, step in ((0, 1), (1, -1)):
                send_block(h, i, 0, 0, h, step)
            for i, step in ((4, 1), (5, -1)):
                send_block(h, i, 0, 0, 1 - h, step)

        def spread(h, j):
            for i, step in ((0, 1), (1, -1)):
                send_block(h, 4 + 4 * j + i, RING[j], 0, 1 - h, step)

        def s1():
            for i in (0, 1):
                o = (-1, 1)[i]
                for h in (0, 1):
                    wait(h, i, o, 0)
                    send_block(h, 2 + i, o, 0, h, -o, i)
                for h in (0, 1):
                    spread(h, 1 + i)

        def relay(j):
            for i in (0, 1):
                o = (-1, 1)[i]
                for h in (1, 0):
                    wait(h, 4 + 4 * j + i, RING[j], o)
                    send_block(h, 6 + 4 * j + i, RING[j], o, 1 - h, -o, i)

        def s3():
            for h in (0, 1):
                wait(h, 2, 2, 0, 0)
                wait(h, 3, 2, 0, 1)
                spread(h, 3)

        def finish():
            for j in range(4):
                for h in (0, 1):
                    for i in (0, 1):
                        wait(h, 6 + 4 * j + i, RING[j], 2, i)

        return own, s1, relay, s3, finish

    def reduce(buf, in1, in2, res, which):
        send = rs_send.at[which]
        order = (3, 2, 1, 0)

        def sem(h, j, i):
            return rs_recv.at[which * 60 + h * 30 + j * 6 + i]

        def piece(h, fst, snd, q=None):
            o = coord(h, fst, snd)
            first = h * half + (0 if q is None else q * quarter)
            return buf.at[flat(*o), pl.ds(first, half if q is None else quarter)]

        def land(h, j, first, n):
            if j < 4:
                return in1.at[h, j, pl.ds(first, n)]
            return in2.at[h, pl.ds(first, n)]

        def term(h, j, k, q=None):
            if j < 4:
                return piece(h, RING[j], k, q)
            return piece(h, k, 0, q)

        q1, q2, fp, fm = 0, quarter, half, 2 * half

        def axis_of(h, j):
            return 1 - h if j < 4 else h

        def init(h, j):
            ax = axis_of(h, j)
            put(term(h, j, 2, 0), land(h, j, q1, quarter), send, sem(h, j, 0), ax, 1)
            put(term(h, j, 2, 1), land(h, j, q2, quarter), send, sem(h, j, 1), ax, -1)
            put(term(h, j, 1, 1), land(h, j, fp + quarter, quarter), send, sem(h, j, 2), ax, 1)
            put(term(h, j, -1, 0), land(h, j, fm, quarter), send, sem(h, j, 3), ax, -1)

        def comb(h, j):
            ax = axis_of(h, j)
            for i, k, first, dst in ((0, 1, q1, fp), (1, -1, q2, fm + quarter)):
                r = land(h, j, first, quarter)
                wait_bytes(r, sem(h, j, i))
                r[...] = (r[...].astype(F32) + term(h, j, k, i)[...].astype(F32)).astype(BF)
                put(r, land(h, j, dst, quarter), send, sem(h, j, 4 + i), ax, k)

        def fin(h, j):
            for first, i in ((fp + quarter, 2), (fm, 3), (fp, 4), (fm + quarter, 5)):
                wait_bytes(land(h, j, first, quarter), sem(h, j, i))
            own = term(h, j, 0)
            total = (
                own[...].astype(F32)
                + land(h, j, fp, half)[...].astype(F32)
                + land(h, j, fm, half)[...].astype(F32)
            ).astype(BF)
            if j < 4:
                own[...] = total
            else:
                res[pl.ds(h * half, half)] = total

        return init, comb, fin

    own, s1, relay, s3, finish = gather(tok_all, 0)
    for h in (0, 1):
        wait_bytes(tok_all.at[f, pl.ds(h * half, half)], a2a_recv.at[h])
        own(h)
    s1()
    relay(0)
    s3()
    relay(1)
    relay(2)
    relay(3)
    own2, s1b, relay2, s3b, finish2 = gather(grad_all, 1)
    for h in (0, 1):
        wait_bytes(grad_all.at[f, pl.ds(h * half, half)], a2a_recv.at[2 + h])
        own2(h)
    finish()

    n_pair = tok_all.shape[0] // 2
    low = lax.broadcasted_iota(jnp.int32, (rows, 128), 1) < 64
    for load in loads:
        load.wait()

    def span(p, size=pair):
        return pl.ds(pl.multiple_of(p * pair, 128), size)

    def tok_pair(p):
        return jnp.concatenate(
            [tok_all[2 * p, :, :main], tok_rem[p], tok_all[2 * p + 1, :, :main]], axis=1
        )

    def grad_pair(p):
        return jnp.concatenate([grad_all[2 * p], grad_rem[p], grad_all[2 * p + 1]], axis=1)

    pre[...] = jnp.zeros_like(pre)
    gh[...] = jnp.zeros_like(gh)

    @pl.loop(0, n_pair)
    def _(p):
        even = tok_all[2 * p, :, main:].astype(F32)
        other = tok_all[2 * p + 1, :, main:].astype(F32)
        tok_rem[p] = jnp.where(low, even, other).astype(BF)
        grad_rem[p] = pltpu.roll(jnp.where(low, other, even), 64, 1).astype(BF)
        both = jnp.concatenate([gate[span(p)], up[span(p)]], axis=1)
        pre[...] += dot(tok_pair(p), both)

    pg = pre[:, :128]
    pu = pre[:, 128:]
    sg = jax.nn.sigmoid(pg)
    hid[...] = (pg * sg * pu).astype(BF)
    s1b()
    relay2(0)

    @pl.loop(0, n_pair)
    def _(p):
        o = dot(hid[...], down[:, span(p)]).astype(BF)
        out_part[2 * p] = o[:, :main]
        out_rem[p] = o[:, main:wide]
        out_part[2 * p + 1] = o[:, wide:]

    s3b()
    relay2(1)
    relay2(2)
    relay2(3)
    init, comb, fin = reduce(out_part, out_in, out_in2, out_res, 0)
    for j in (3, 2, 1, 0):
        for h in (0, 1):
            init(h, j)
    finish2()

    @pl.loop(0, n_pair)
    def _(p):
        gh[...] += dot(grad_pair(p), down[:, span(p)], LAST)

    pg = pre[:, :128]
    pu = pre[:, 128:]
    sg = jax.nn.sigmoid(pg)
    gpre[:, :128] = (gh[...] * pu * sg * (1.0 + pg * (1.0 - sg))).astype(BF)
    gpre[:, 128:] = (gh[...] * (pg * sg)).astype(BF)
    for j in (3, 2):
        for h in (0, 1):
            comb(h, j)

    @pl.loop(0, n_pair)
    def _(p):
        both = jnp.concatenate([gate[span(p)], up[span(p)]], axis=1)
        r = dot(gpre[...], both, LAST)
        ret_part[2 * p, :, :main] = r[:, :main].astype(BF)
        ret_part[2 * p + 1, :, :main] = r[:, wide:].astype(BF)
        rem = pltpu.roll(r[:, main:wide], 64, 1)
        o = out_rem[p].astype(F32)
        ret_part[2 * p, :, main:] = jnp.where(low, o, rem).astype(BF)
        ret_part[2 * p + 1, :, main:] = jnp.where(low, rem, o).astype(BF)

    for j in (1, 0):
        for h in (0, 1):
            comb(h, j)
    for j in (3, 2, 1):
        for h in (0, 1):
            fin(h, j)
    for h in (0, 1):
        init(h, 4)
    init2, comb2, fin2 = reduce(ret_part, ret_in, ret_in2, ret_res, 1)
    for j in (3, 2, 1, 0):
        for h in (0, 1):
            init2(h, j)
    for h in (0, 1):
        fin(h, 0)
        comb(h, 4)

    @pl.loop(0, n_pair)
    def _(p):
        gdown[:, span(p)] = dot(hid[...], grad_pair(p), ROWS).astype(BF)

    for h in (0, 1):
        fin(h, 4)
    scatter(out_res, lambda r: out_back.at[pl.ds(r, slot)], back_send.at[0], back_recv.at[0])
    for j in (3, 2):
        for h in (0, 1):
            comb2(h, j)

    @pl.loop(0, n_pair)
    def _(p):
        g = dot(tok_pair(p), gpre[...], ROWS).astype(BF)
        ggate[span(p)] = g[:, :128]
        gup[span(p)] = g[:, 128:]

    stores = [
        pltpu.make_async_copy(src, dst, gout_sem.at[i])
        for i, (src, dst) in enumerate(((ggate, ggate_hbm), (gup, gup_hbm), (gdown, gdown_hbm)))
    ]
    for store in stores:
        store.start()
    for j in (1, 0):
        for h in (0, 1):
            comb2(h, j)
    for j in (3, 2, 1):
        for h in (0, 1):
            fin2(h, j)
    for h in (0, 1):
        init2(h, 4)
    for h in (0, 1):
        comb2(h, 4)
    for h in (0, 1):
        fin2(h, 0)
    for h in (0, 1):
        fin2(h, 4)
    scatter(ret_res, lambda r: ret_back.at[pl.ds(r, slot)], back_send.at[1], back_recv.at[1])

    there = lax.broadcasted_iota(jnp.int32, (n_tok, rows), 0) == row_idx_ref[...]
    place = jnp.where(there, 1.0, 0.0).astype(BF)
    wait_bytes(out_back, back_recv.at[0])
    wait_bytes(ret_back, back_recv.at[1])
    unpack_a = packing(448 * odd, 384 + 64 * odd)
    unpack_b = packing(64 + 320 * odd, 448 - 64 * odd)
    out_rows = jnp.concatenate([out_back[...], ret_back[:, main:]], axis=1)
    scaled = dot(out_rows, unpack_a, LAST) * w_ref[...]
    high = scaled.astype(BF)
    rest = (scaled - high.astype(F32)).astype(BF)
    mixture_ref[...] = (dot(place, high) + dot(place, rest)).astype(BF)
    ret_rows = dot(ret_back[...], unpack_b, LAST).astype(BF)
    grad_tok_ref[...] = dot(place, ret_rows).astype(BF)

    wait_bytes(tok_loc.at[pl.ds(0, rows - slot)], a2a_send.at[0])
    wait_bytes(grad_loc.at[pl.ds(0, rows - slot)], a2a_send.at[1])
    wait_bytes(tok_all.at[pl.ds(0, 15)], ag_send.at[0])
    wait_bytes(grad_all.at[pl.ds(0, 15)], ag_send.at[1])
    wait_bytes(out_part.at[pl.ds(0, 15)], rs_send.at[0])
    wait_bytes(ret_part.at[pl.ds(0, 15)], rs_send.at[1])
    wait_bytes(out_res.at[pl.ds(0, rows - slot)], back_send.at[0])
    wait_bytes(ret_res.at[pl.ds(0, rows - slot)], back_send.at[1])
    for store in stores:
        store.wait()


def per_device(tokens, cotangent, gate_weight, up_weight, down_weight, chosen, counts, gate_prob):
    experts, _, slots = chosen.shape
    n_tok, feats = tokens.shape
    rows = experts * slots
    width = gate_weight.shape[1]
    hidden = gate_weight.shape[2]
    wide, main = 512, 384
    n = width // feats
    position = lax.broadcasted_iota(jnp.int32, (experts, slots), 1)
    live = position < counts
    index = jnp.where(live, chosen[:, 0, :], -1)
    weight = jnp.where(live, gate_prob[:, 0, :], 0.0)
    vmem = pl.BlockSpec(memory_space=pltpu.VMEM)
    hbm = pl.BlockSpec(memory_space=pl.ANY)
    dma = pltpu.SemaphoreType.DMA
    half = rows // 2
    outs = pl.pallas_call(
        kernel,
        out_shape=(
            jax.ShapeDtypeStruct((n_tok, feats), BF),
            jax.ShapeDtypeStruct((n_tok, feats), BF),
            jax.ShapeDtypeStruct((width, hidden), BF),
            jax.ShapeDtypeStruct((width, hidden), BF),
            jax.ShapeDtypeStruct((hidden, width), BF),
        ),
        in_specs=[vmem] * 5 + [hbm] * 3,
        out_specs=(vmem, vmem, hbm, hbm, hbm),
        scratch_shapes=[
            pltpu.VMEM((rows, wide), BF),
            pltpu.VMEM((rows, main), BF),
            pltpu.VMEM((n, rows, wide), BF),
            pltpu.VMEM((n, rows, main), BF),
            pltpu.VMEM((n // 2, rows, 128), BF),
            pltpu.VMEM((n // 2, rows, 128), BF),
            pltpu.VMEM((width, hidden), BF),
            pltpu.VMEM((width, hidden), BF),
            pltpu.VMEM((hidden, width), BF),
            pltpu.VMEM((width, hidden), BF),
            pltpu.VMEM((width, hidden), BF),
            pltpu.VMEM((hidden, width), BF),
            pltpu.VMEM((n, rows, main), BF),
            pltpu.VMEM((n // 2, rows, 128), BF),
            pltpu.VMEM((n, rows, wide), BF),
            pltpu.VMEM((rows, 2 * hidden), F32),
            pltpu.VMEM((rows, hidden), F32),
            pltpu.VMEM((rows, hidden), BF),
            pltpu.VMEM((rows, 2 * hidden), BF),
            pltpu.VMEM((2, 4, 3 * half, main), BF),
            pltpu.VMEM((2, 3 * half, main), BF),
            pltpu.VMEM((2, 4, 3 * half, wide), BF),
            pltpu.VMEM((2, 3 * half, wide), BF),
            pltpu.VMEM((rows, main), BF),
            pltpu.VMEM((rows, wide), BF),
            pltpu.VMEM((rows, main), BF),
            pltpu.VMEM((rows, wide), BF),
            dma((3,)),
            dma((2,)),
            dma((4,)),
            dma((2,)),
            dma((80,)),
            dma((2,)),
            dma((120,)),
            dma((2,)),
            dma((2,)),
            dma((3,)),
        ],
        compiler_params=pltpu.CompilerParams(
            collective_id=0, has_side_effects=True, vmem_limit_bytes=60 * 1024 * 1024
        ),
        name="experts",
    )(
        index.reshape(rows, 1),
        index.reshape(1, rows),
        weight.reshape(rows, 1),
        tokens,
        cotangent,
        gate_weight[0],
        up_weight[0],
        down_weight[0],
    )
    mixture, grad_tokens, grad_gate, grad_up, grad_down = outs
    return mixture, grad_tokens, grad_gate[None], grad_up[None], grad_down[None]


def solution(mesh):
    placed = (
        P("ep", "fsdp"),
        P("ep", "fsdp"),
        P("ep", None, "fsdp"),
        P("ep", None, "fsdp"),
        P("ep", "fsdp", None),
        P(None, "ep", None),
        P(None, "ep"),
        P(None, "ep", None),
    )
    return jax.shard_map(
        per_device,
        mesh=mesh,
        in_specs=placed,
        out_specs=(
            P("ep", "fsdp"),
            P("ep", "fsdp"),
            P("ep", None, "fsdp"),
            P("ep", None, "fsdp"),
            P("ep", "fsdp", None),
        ),
        check_vma=False,
    )
```

time: 704 us -> 140 us (0.20)
  waiting for transfers between devices: 545 us -> 0 us
  Pallas kernels: 0 us -> 118 us
  local copies, waits for them, and re-layouts: 68.8 us -> 15 us
  starting transfers between devices: 34.7 us -> 0 us
  matrix products: 31.8 us -> 0 us
  between operations: 13.9 us -> 0.69 us
    all_gather x2 -> x0, waiting for transfers between devices: 328 us -> none  [the longest x1 180 us: per_device(): lax.all_gather(picked_tokens, 'fsdp', axis=2, tiled=True)]
    reduce_scatter x2 -> x0, waiting for transfers between devices: 141 us -> none  [send_back(): lax.psum_scatter(term.astype(jnp.bfloat16), 'fsdp', scatter_dimension=1,...]
    pallas_call x0 -> x1, Pallas kernels: none -> 118 us  [per_device(): pl.pallas_call(kernel, out_shape=(jax.ShapeDtypeStruct((n_tok, feats), BF...]
    all_to_all x4 -> x0, waiting for transfers between devices: 75.2 us -> none  [the longest x1 75.2 us: per_device(): lax.all_to_all(wide_grads, 'ep', split_axis=0, concat_axis=0, tiled=True)]
    all_gather x2 -> x0, local copies, waits for them, and re-layouts: 53.4 us -> none  [the longest x1 26.9 us: per_device(): lax.all_gather(picked_tokens, 'fsdp', axis=2, tiled=True)]
    all_to_all x4 -> x0, starting transfers between devices: 34.6 us -> none  [the longest x2 18.8 us: send_back(): lax.all_to_all(to_slots(summed, experts, slot_count), 'ep', split_axis=0,...]
    dot_general x9 -> x0, matrix products: 31.8 us -> none  [the longest x1 4.44 us: per_device(): lax.dot_general(rows_tokens, grad_pre_up, contract_rows, preferred_elemen...]
    unnamed x18 -> x17, local copies, waits for them, and re-layouts: 4.58 us -> 13.7 us
  transfers between devices with their start and end apart: 8 -> 0, of which waited for: 5 -> 0; matrix products, arithmetic and copies ran while one was open for 13% -> 0% of each run, Pallas kernels for 0% -> 0%
where the time goes in v1:
time: 140 us; the launch traced here: 139 us
  Pallas kernels  118 us (84%)
  local copies, waits for them, and re-layouts  15 us (11%)
  other arithmetic  5.38 us (4%)
    pallas_call x1, Pallas kernels, per_device(): pl.pallas_call(kernel, out_shape=(jax.ShapeDtypeStruct((n_tok, feats), BF...  118 us
    unnamed x17, local copies, waits for them, and re-layouts  13.7 us

profile of v1, /device:TPU:1, one launch (start us, length us, event | category | flops | bytes accessed | tf_op | source)
XLA Modules:
  0.0 139.1 jit_solution(8690660430266162799)
XLA Ops:
  0.6 0.8 squeeze.18
  1.5 0.7 iota_compare_fusion
  2.2 0.1 lt.38
  2.3 0.6 broadcast_select_fusion.2.row_idx_ref
  2.9 0.5 broadcast.45
  3.4 1.4 reduce.9
  4.7 0.5 broadcast.44
  5.3 1.4 reduce.8
  6.6 0.1 lt.39
  6.8 0.1 squeeze.23
  6.9 0.7 broadcast_select_fusion.1.idx_ref
  7.5 0.1 squeeze.24
  7.6 0.7 broadcast_select_fusion.w_ref
  8.3 2.0 %copy.21.tok_ref = bf16[512,448]{1,0:T(8,128)(2,1)} copy(bf16[512,448]{0,1:T(8,128)(2,1)} %param.8) | data formatting | bytes 917504 | tf_op args[0]
  10.3 1.0 copy.22.cot_ref
  11.3 118.1 %experts.1 = (bf16[512,448]{1,0:T(8,128)(2,1)}, bf16[512,448]{1,0:T(8,128)(2,1)}, bf16[7168,128]{1,0:T(8,128)(2,1)}, bf16[7168,128]{1,0:T(8,128)(2,1)}, bf16[128,7168]{1,0:T(8,128)(2,1)}) custom-call(s32[256,1]{1,0:T(8,128)} %broadcast_select_fusion.1.idx_ref, s32[1,256]{1,0:T(1,128)} %broadcast_select_fusion.2.row_idx_ref, ...), custom_call_target="tpu_custom_call" | custom-call | tf_op jit(solution)/shard_map/experts/pallas_call | solution.py:421
  129.4 0.0 copy-start.2
  129.4 2.1 %copy.23 = bf16[512,448]{0,1:T(8,128)(2,1)} copy(bf16[512,448]{1,0:T(8,128)(2,1)} %get-tuple-element.20) | data formatting | bytes 917504
  131.5 2.0 %copy.24 = bf16[512,448]{0,1:T(8,128)(2,1)} copy(bf16[512,448]{1,0:T(8,128)(2,1)} %get-tuple-element.21) | data formatting | bytes 917504
  133.5 1.2 copy.28
  134.8 0.9 copy-done.1
  135.7 1.2 copy.29
  136.9 0.9 copy-done
  137.9 1.2 copy.30
  (5 shorter events, 0.0 us)
Async XLA Ops:
  0.6 9.7 %copy-start.3 = (bf16[512,448]{0,1:T(8,128)(2,1)S(1)}, bf16[512,448]{0,1:T(8,128)(2,1)}, u32[]{:S(2)}) copy-start(bf16[512,448]{0,1:T(8,128)(2,1)} %param.9) | copy-start | bytes 1376260
  129.4 4.2 %copy-start.2 = (bf16[7168,128]{1,0:T(8,128)(2,1)S(1)}, bf16[7168,128]{1,0:T(8,128)(2,1)}, u32[]{:S(2)}) copy-start(bf16[7168,128]{1,0:T(8,128)(2,1)} %get-tuple-element.12) | copy-start | bytes 5505028
  133.5 2.2 %copy-start.1 = (bf16[7168,128]{1,0:T(8,128)(2,1)S(1)}, bf16[7168,128]{1,0:T(8,128)(2,1)}, u32[]{:S(2)}) copy-start(bf16[7168,128]{1,0:T(8,128)(2,1)} %get-tuple-element.13) | copy-start | bytes 5505028
  135.7 2.2 %copy-start = (bf16[128,7168]{1,0:T(8,128)(2,1)S(1)}, bf16[128,7168]{1,0:T(8,128)(2,1)}, u32[]{:S(2)}) copy-start(bf16[128,7168]{1,0:T(8,128)(2,1)} %get-tuple-element.14) | copy-start | bytes 5505028

commit v2 on v1

--- a/solution.py
+++ b/solution.py
@@ -18,18 +18,30 @@
     return lax.dot_general(a, b, dims, preferred_element_type=F32)
 
 
+def packings(odd, feats, main, wide):
+    fi = lax.broadcasted_iota(jnp.int32, (feats, wide), 0)
+    fj = lax.broadcasted_iota(jnp.int32, (feats, wide), 1)
+
+    def packing(delta, low):
+        body = (fi == fj + 64 * odd) & (fj < main)
+        tail = (fi == fj - delta) & (fj >= low) & (fj < low + 64)
+        return jnp.where(body | tail, 1.0, 0.0).astype(BF)
+
+    return packing(448 * odd, 384 + 64 * odd), packing(64 + 320 * odd, 448 - 64 * odd)
+
+
 def kernel(
-    idx_ref, row_idx_ref, w_ref, tok_ref, cot_ref, gate_hbm, up_hbm, down_hbm,
-    mixture_ref, grad_tok_ref, ggate_hbm, gup_hbm, gdown_hbm,
+    count_ref, chosen_ref, prob_ref, tok_ref, cot_ref, gate_hbm, up_hbm, down_hbm,
+    out_back, ret_back, hot_ref, w_ref, ggate, gup, gdown,
     tok_loc, grad_loc, tok_all, grad_all, tok_rem, grad_rem,
-    gate, up, down, ggate, gup, gdown,
+    gate, up, down,
     out_part, out_rem, ret_part, pre, gh, hid, gpre,
-    out_in, out_in2, ret_in, ret_in2, out_res, ret_res, out_back, ret_back,
-    w_sem, a2a_send, a2a_recv, ag_send, ag_recv, rs_send, rs_recv, back_send, back_recv, gout_sem,
+    out_in, out_in2, ret_in, ret_in2, out_res, ret_res,
+    w_sem, a2a_send, a2a_recv, ag_send, ag_recv, rs_send, rs_recv, back_send, back_recv,
 ):
     f = lax.axis_index("fsdp")
     me = lax.axis_index("ep")
-    n_ep = idx_ref.shape[0] // 16
+    n_ep = chosen_ref.shape[0]
     y = lax.div(f, SIDE)
     x = lax.rem(f, SIDE)
     odd = lax.rem(x, 2)
@@ -38,7 +50,7 @@
     rows = tok_all.shape[1]
     half = rows // 2
     quarter = rows // 4
-    feats = tok_ref.shape[1]
+    feats = tok_ref.shape[0]
     pair = 2 * feats
     slot = 16
 
@@ -63,21 +75,25 @@
     for load in loads:
         load.start()
 
-    n_tok = tok_ref.shape[0]
-    fi = lax.broadcasted_iota(jnp.int32, (feats, wide), 0)
-    fj = lax.broadcasted_iota(jnp.int32, (feats, wide), 1)
-
-    def packing(delta, low):
-        body = (fi == fj + 64 * odd) & (fj < main)
-        tail = (fi == fj - delta) & (fj >= low) & (fj < low + 64)
-        return jnp.where(body | tail, 1.0, 0.0).astype(BF)
-
-    pack_a = packing(448 * odd, 384 + 64 * odd)
-    pack_b = packing(64 + 320 * odd, 448 - 64 * odd)
-    hit = lax.broadcasted_iota(jnp.int32, (rows, n_tok), 1) == idx_ref[...]
+    n_tok = tok_ref.shape[1]
+    pack_a, pack_b = packings(odd, feats, main, wide)
+    j = lax.broadcasted_iota(jnp.int32, (1, slot), 1)
+    index, weight = [], []
+    for e in range(n_ep):
+        live = j < count_ref[e]
+        index.append(jnp.broadcast_to(jnp.where(live, chosen_ref[e : e + 1], -1), (slot, slot)))
+        weight.append(jnp.broadcast_to(jnp.where(live, prob_ref[e : e + 1], 0.0), (slot, slot)))
+    shape = (rows, slot)
+    mine = lax.rem(lax.broadcasted_iota(jnp.int32, shape, 0), slot) == lax.broadcasted_iota(jnp.int32, shape, 1)
+    index = jnp.concatenate(index, axis=0).astype(F32)
+    index = jnp.sum(jnp.where(mine, index, 0.0), axis=1, keepdims=True).astype(jnp.int32)
+    weight = jnp.concatenate(weight, axis=0)
+    w_ref[...] = jnp.sum(jnp.where(mine, weight, 0.0), axis=1, keepdims=True)
+    hit = lax.broadcasted_iota(jnp.int32, (rows, n_tok), 1) == index
     onehot = jnp.where(hit, 1.0, 0.0).astype(BF)
-    tp = dot(dot(onehot, tok_ref[...]).astype(BF), pack_a)
-    gp = dot((dot(onehot, cot_ref[...]) * w_ref[...]).astype(BF), pack_b)
+    hot_ref[...] = onehot
+    tp = dot(dot(onehot, tok_ref[...], LAST).astype(BF), pack_a)
+    gp = dot((dot(onehot, cot_ref[...], LAST) * w_ref[...]).astype(BF), pack_b)
     tok_loc[:, :main] = tp[:, :main].astype(BF)
     tok_loc[:, main:] = (tp[:, main:] + gp[:, main:]).astype(BF)
     grad_loc[...] = gp[:, :main].astype(BF)
@@ -354,12 +370,6 @@
         ggate[span(p)] = g[:, :128]
         gup[span(p)] = g[:, 128:]
 
-    stores = [
-        pltpu.make_async_copy(src, dst, gout_sem.at[i])
-        for i, (src, dst) in enumerate(((ggate, ggate_hbm), (gup, gup_hbm), (gdown, gdown_hbm)))
-    ]
-    for store in stores:
-        store.start()
     for j in (1, 0):
         for h in (0, 1):
             comb2(h, j)
@@ -376,19 +386,8 @@
         fin2(h, 4)
     scatter(ret_res, lambda r: ret_back.at[pl.ds(r, slot)], back_send.at[1], back_recv.at[1])
 
-    there = lax.broadcasted_iota(jnp.int32, (n_tok, rows), 0) == row_idx_ref[...]
-    place = jnp.where(there, 1.0, 0.0).astype(BF)
     wait_bytes(out_back, back_recv.at[0])
     wait_bytes(ret_back, back_recv.at[1])
-    unpack_a = packing(448 * odd, 384 + 64 * odd)
-    unpack_b = packing(64 + 320 * odd, 448 - 64 * odd)
-    out_rows = jnp.concatenate([out_back[...], ret_back[:, main:]], axis=1)
-    scaled = dot(out_rows, unpack_a, LAST) * w_ref[...]
-    high = scaled.astype(BF)
-    rest = (scaled - high.astype(F32)).astype(BF)
-    mixture_ref[...] = (dot(place, high) + dot(place, rest)).astype(BF)
-    ret_rows = dot(ret_back[...], unpack_b, LAST).astype(BF)
-    grad_tok_ref[...] = dot(place, ret_rows).astype(BF)
 
     wait_bytes(tok_loc.at[pl.ds(0, rows - slot)], a2a_send.at[0])
     wait_bytes(grad_loc.at[pl.ds(0, rows - slot)], a2a_send.at[1])
@@ -398,6 +397,31 @@
     wait_bytes(ret_part.at[pl.ds(0, 15)], rs_send.at[1])
     wait_bytes(out_res.at[pl.ds(0, rows - slot)], back_send.at[0])
     wait_bytes(ret_res.at[pl.ds(0, rows - slot)], back_send.at[1])
+
+
+def finish_kernel(
+    out_ref, ret_ref, hot_ref, w_ref, ggate, gup, gdown,
+    mixture_ref, grad_tok_ref, ggate_hbm, gup_hbm, gdown_hbm, sem,
+):
+    stores = [
+        pltpu.make_async_copy(src, dst, sem.at[i])
+        for i, (src, dst) in enumerate(((ggate, ggate_hbm), (gup, gup_hbm), (gdown, gdown_hbm)))
+    ]
+    for store in stores:
+        store.start()
+    odd = lax.rem(lax.axis_index("fsdp"), 2)
+    feats = mixture_ref.shape[0]
+    main, wide = out_ref.shape[1], ret_ref.shape[1]
+    unpack_a, unpack_b = packings(odd, feats, main, wide)
+    out_rows = jnp.concatenate([out_ref[...], ret_ref[:, main:]], axis=1)
+    scaled = out_rows.astype(F32) * w_ref[...]
+    high = scaled.astype(BF)
+    rest = (scaled - high.astype(F32)).astype(BF)
+    hot = hot_ref[...]
+    high = dot(unpack_a, high, LAST).astype(BF)
+    rest = dot(unpack_a, rest, LAST).astype(BF)
+    mixture_ref[...] = (dot(high, hot) + dot(rest, hot)).astype(BF)
+    grad_tok_ref[...] = dot(dot(unpack_b, ret_ref[...], LAST).astype(BF), hot).astype(BF)
     for store in stores:
         store.wait()
 
@@ -410,25 +434,24 @@
     hidden = gate_weight.shape[2]
     wide, main = 512, 384
     n = width // feats
-    position = lax.broadcasted_iota(jnp.int32, (experts, slots), 1)
-    live = position < counts
-    index = jnp.where(live, chosen[:, 0, :], -1)
-    weight = jnp.where(live, gate_prob[:, 0, :], 0.0)
     vmem = pl.BlockSpec(memory_space=pltpu.VMEM)
+    smem = pl.BlockSpec(memory_space=pltpu.SMEM)
     hbm = pl.BlockSpec(memory_space=pl.ANY)
     dma = pltpu.SemaphoreType.DMA
     half = rows // 2
-    outs = pl.pallas_call(
+    kept = pl.pallas_call(
         kernel,
         out_shape=(
-            jax.ShapeDtypeStruct((n_tok, feats), BF),
-            jax.ShapeDtypeStruct((n_tok, feats), BF),
-            jax.ShapeDtypeStruct((width, hidden), BF),
-            jax.ShapeDtypeStruct((width, hidden), BF),
-            jax.ShapeDtypeStruct((hidden, width), BF),
+            pltpu.VMEM((rows, main), BF),
+            pltpu.VMEM((rows, wide), BF),
+            pltpu.VMEM((rows, n_tok), BF),
+            pltpu.VMEM((rows, 1), F32),
+            pltpu.VMEM((width, hidden), BF),
+            pltpu.VMEM((width, hidden), BF),
+            pltpu.VMEM((hidden, width), BF),
         ),
-        in_specs=[vmem] * 5 + [hbm] * 3,
-        out_specs=(vmem, vmem, hbm, hbm, hbm),
+        in_specs=[smem] + [vmem] * 4 + [hbm] * 3,
+        out_specs=(vmem,) * 7,
         scratch_shapes=[
             pltpu.VMEM((rows, wide), BF),
             pltpu.VMEM((rows, main), BF),
@@ -436,9 +459,6 @@
             pltpu.VMEM((n, rows, main), BF),
             pltpu.VMEM((n // 2, rows, 128), BF),
             pltpu.VMEM((n // 2, rows, 128), BF),
-            pltpu.VMEM((width, hidden), BF),
-            pltpu.VMEM((width, hidden), BF),
-            pltpu.VMEM((hidden, width), BF),
             pltpu.VMEM((width, hidden), BF),
             pltpu.VMEM((width, hidden), BF),
             pltpu.VMEM((hidden, width), BF),
@@ -455,8 +475,6 @@
             pltpu.VMEM((2, 3 * half, wide), BF),
             pltpu.VMEM((rows, main), BF),
             pltpu.VMEM((rows, wide), BF),
-            pltpu.VMEM((rows, main), BF),
-            pltpu.VMEM((rows, wide), BF),
             dma((3,)),
             dma((2,)),
             dma((4,)),
@@ -466,24 +484,37 @@
             dma((120,)),
             dma((2,)),
             dma((2,)),
-            dma((3,)),
         ],
         compiler_params=pltpu.CompilerParams(
-            collective_id=0, has_side_effects=True, vmem_limit_bytes=60 * 1024 * 1024
+            collective_id=0, has_side_effects=True, vmem_limit_bytes=52 * 1024 * 1024
         ),
         name="experts",
     )(
-        index.reshape(rows, 1),
-        index.reshape(1, rows),
-        weight.reshape(rows, 1),
-        tokens,
-        cotangent,
+        counts[:, 0],
+        chosen[:, 0, :],
+        gate_prob[:, 0, :],
+        tokens.T,
+        cotangent.T,
         gate_weight[0],
         up_weight[0],
         down_weight[0],
     )
-    mixture, grad_tokens, grad_gate, grad_up, grad_down = outs
-    return mixture, grad_tokens, grad_gate[None], grad_up[None], grad_down[None]
+    mixture, grad_tokens, grad_gate, grad_up, grad_down = pl.pallas_call(
+        finish_kernel,
+        out_shape=(
+            jax.ShapeDtypeStruct((feats, n_tok), BF),
+            jax.ShapeDtypeStruct((feats, n_tok), BF),
+            jax.ShapeDtypeStruct((width, hidden), BF),
+            jax.ShapeDtypeStruct((width, hidden), BF),
+            jax.ShapeDtypeStruct((hidden, width), BF),
+        ),
+        in_specs=[vmem] * 7,
+        out_specs=(vmem, vmem, hbm, hbm, hbm),
+        scratch_shapes=[dma((3,))],
+        compiler_params=pltpu.CompilerParams(vmem_limit_bytes=16 * 1024 * 1024),
+        name="finish",
+    )(*kept)
+    return mixture.T, grad_tokens.T, grad_gate[None], grad_up[None], grad_down[None]
 
 
 def solution(mesh):

time: 140 us -> 121 us (0.86)
  local copies, waits for them, and re-layouts: 15 us -> 0 us
  other arithmetic: 5.38 us -> 0 us
  Pallas kernels: 118 us -> 120 us
    unnamed x17 -> x0, local copies, waits for them, and re-layouts: 13.7 us -> none
    unnamed x2 -> x0, other arithmetic: 2.73 us -> none
    select_n x3 -> x0, other arithmetic: 1.91 us -> none  [the longest x2 1.24 us: per_device(): index = jnp.where(live, chosen[:, 0, :], -1)]
    pallas_call x1 -> x2, Pallas kernels: 118 us -> 120 us  [the longest x1 116 us: per_device(): pl.pallas_call(kernel, out_shape=(pltpu.VMEM((rows, main), BF), pltpu.VME...]
where the time goes in v2:
time: 121 us; the launch traced here: 120 us
  Pallas kernels  120 us (99%)
    pallas_call x1, Pallas kernels, per_device(): pl.pallas_call(kernel, out_shape=(pltpu.VMEM((rows, main), BF), pltpu.VME...  116 us
    pallas_call x1, Pallas kernels, per_device(): pl.pallas_call(finish_kernel, out_shape=(jax.ShapeDtypeStruct((feats, n_t...  3.71 us

profile of v2, /device:TPU:1, one launch (start us, length us, event | category | flops | bytes accessed | tf_op | source)
XLA Modules:
  0.0 120.5 jit_solution(221679746638255867)
XLA Ops:
  0.6 116.1 %experts.1 = (bf16[256,384]{1,0:T(8,128)(2,1)S(1)}, bf16[256,512]{1,0:T(8,128)(2,1)S(1)}, bf16[256,512]{1,0:T(8,128)(2,1)S(1)}, f32[256,1]{1,0:T(8,128)S(1)}, bf...) custom-call(s32[16]{0:T(128)} %bitcast.20, s32[16,16]{1,0:T(8,128)} %bitcast.18, ...), custom_call_target="tpu_custom_call" | custom-call | tf_op jit(solution)/shard_map/experts/pallas_call | solution.py:442
  116.7 3.7 %finish.1 = (bf16[448,512]{1,0:T(8,128)(2,1)}, bf16[448,512]{1,0:T(8,128)(2,1)}, bf16[7168,128]{1,0:T(8,128)(2,1)}, bf16[7168,128]{1,0:T(8,128)(2,1)}, bf16[128,7168]{1,0:T(8,128)(2,1)}) custom-call(bf16[256,384]{1,0:T(8,128)(2,1)S(1)} %get-tuple-element.17.out_ref, bf16[256,512]{1,0:T(8,128)(2,1)S(1)} %get-tuple-element.18.ret_ref, ...), custom_call_target="tpu_custom_call" | custom-call | tf_op jit(solution)/shard_map/finish/pallas_call | solution.py:502

commit v3 on v2

v3 whole, which is shorter than its diff:
```python
import jax
import jax.numpy as jnp
from jax import lax
from jax.experimental import pallas as pl
from jax.experimental.pallas import tpu as pltpu
from jax.sharding import PartitionSpec as P

MESH = pl.DeviceIdType.MESH
BF = jnp.bfloat16
F32 = jnp.float32
SIDE = 4
RING = (0, -1, 1, 2)
LAST = (((1,), (1,)), ((), ()))
ROWS = (((0,), (0,)), ((), ()))


def dot(a, b, dims=(((1,), (0,)), ((), ()))):
    return lax.dot_general(a, b, dims, preferred_element_type=F32)


def packings(odd, feats, main, wide):
    fi = lax.broadcasted_iota(jnp.int32, (feats, main), 0)
    fj = lax.broadcasted_iota(jnp.int32, (feats, main), 1)
    body = jnp.where(fi - fj == 64 * odd, 1.0, 0.0)
    ti = lax.broadcasted_iota(jnp.int32, (feats, wide - main), 0)
    tj = lax.broadcasted_iota(jnp.int32, (feats, wide - main), 1)
    where = jnp.where(odd == 1, ti, ti - main)

    def packing(low):
        tail = jnp.where((tj - where == low) & (tj >= low) & (tj < low + 64), 1.0, 0.0)
        return jnp.concatenate([body, tail], axis=1).astype(BF)

    return packing(64 * odd), packing(64 - 64 * odd)


def kernel(
    count_ref, chosen_ref, prob_ref, tok_ref, cot_ref, gate_hbm, up_hbm, down_hbm,
    mixture_ref, grad_tok_ref, ggate, gup, gdown,
    out_back, ret_back, hot_ref, w_ref, pack_ref,
    tok_loc, grad_loc, tok_all, grad_all, tok_rem, grad_rem,
    gate, up, down, down_ring, down_relay, gd_part, gd_relay,
    hid, hid_t, hid_g, gh_send, gh_own, gh_in, pre, gpre,
    out_part, ret_part, out_in, ret_in, ret_in2, out_res, ret_res,
    w_sem, a2a_send, a2a_recv, ag_send, ag_recv, rs_send, rs_recv, out_recv, back_send, back_recv,
    swap_send, swap_recv, small_send, small_recv,
):
    f = lax.axis_index("fsdp")
    me = lax.axis_index("ep")
    n_ep = chosen_ref.shape[0]
    y = lax.div(f, SIDE)
    x = lax.rem(f, SIDE)
    odd = lax.rem(x, 2)
    wide = tok_all.shape[2]
    main = grad_all.shape[2]
    rows = tok_all.shape[1]
    half = rows // 2
    quarter = rows // 4
    feats = tok_ref.shape[0]
    pair = 2 * feats
    slot = 16
    unit = 64

    def flat(dy, dx):
        return lax.rem(y + dy + SIDE, SIDE) * SIDE + lax.rem(x + dx + SIDE, SIDE)

    def coord(axis, along, other=0):
        return (other, along) if axis == 0 else (along, other)

    def place(o):
        return RING.index(o)

    barrier = pltpu.get_barrier_semaphore()
    for axis in (0, 1):
        for o in (1, -1, 2):
            pl.semaphore_signal(barrier, inc=1, device_id={"fsdp": flat(*coord(axis, o))}, device_id_type=MESH)

    @pl.loop(1, n_ep)
    def _(k):
        pl.semaphore_signal(barrier, inc=1, device_id={"ep": lax.rem(me + k, n_ep)}, device_id_type=MESH)

    loads = [
        pltpu.make_async_copy(src, dst, w_sem.at[i])
        for i, (src, dst) in enumerate(((down_hbm, down), (gate_hbm, gate), (up_hbm, up)))
    ]
    for load in loads:
        load.start()

    def wait_bytes(ref, sem):
        pltpu.make_async_copy(ref, ref, sem).wait()

    def put(src, dst, send, recv, axis, step):
        pltpu.make_async_remote_copy(
            src_ref=src, dst_ref=dst, send_sem=send, recv_sem=recv,
            device_id={"fsdp": flat(*coord(axis, step))}, device_id_type=MESH,
        ).start()

    def lanes(h, along, other):
        slice_ = flat(*coord(h, along, other))
        first = pair * lax.div(slice_, 2) + wide * lax.rem(slice_, 2)
        return pl.ds(pl.multiple_of(first, 128), main)

    def owned(ref, h, along, other):
        return ref.at[pl.ds(h * unit, unit), lanes(h, along, other)]

    def block(i):
        return pl.ds(i * unit, unit)

    n_tok = tok_ref.shape[1]
    pack_a, pack_b = packings(odd, feats, main, wide)
    pack_ref[0] = pack_a
    pack_ref[1] = pack_b
    j = lax.broadcasted_iota(jnp.int32, (1, slot), 1)
    index, weight = [], []
    for e in range(n_ep):
        live = j < count_ref[e]
        index.append(jnp.broadcast_to(jnp.where(live, chosen_ref[e : e + 1], -1), (slot, slot)))
        weight.append(jnp.broadcast_to(jnp.where(live, prob_ref[e : e + 1], 0.0), (slot, slot)))
    shape = (rows, slot)
    mine = lax.rem(lax.broadcasted_iota(jnp.int32, shape, 0), slot) == lax.broadcasted_iota(jnp.int32, shape, 1)
    index = jnp.concatenate(index, axis=0).astype(F32)
    index = jnp.sum(jnp.where(mine, index, 0.0), axis=1, keepdims=True).astype(jnp.int32)
    weight = jnp.concatenate(weight, axis=0)
    w_ref[...] = jnp.sum(jnp.where(mine, weight, 0.0), axis=1, keepdims=True)
    hit = lax.broadcasted_iota(jnp.int32, (rows, n_tok), 1) == index
    onehot = jnp.where(hit, 1.0, 0.0).astype(BF)
    hot_ref[...] = onehot

    loads[0].wait()
    pl.semaphore_wait(barrier, n_ep + 5)

    for i in (0, 1):
        for h in (0, 1):
            for d, step in ((0, 1), (1, -1)):
                put(owned(down, h, 2, RING[2 * d + i]), down_relay.at[h, d, i],
                    swap_send.at[0], swap_recv.at[2 * h + d], h, step)
    for c in range(4):
        for h in (0, 1):
            for step in (1, -1):
                put(owned(down, h, step, RING[c]), down_ring.at[h, c, block(place(-step))],
                    swap_send.at[0], swap_recv.at[4 + h], h, step)


    tp = dot(dot(onehot, tok_ref[...], LAST).astype(BF), pack_a)
    gp = dot((dot(onehot, cot_ref[...], LAST) * w_ref[...]).astype(BF), pack_b)
    tok_loc[:, :main] = tp[:, :main].astype(BF)
    tok_loc[:, main:] = (tp[:, main:] + gp[:, main:]).astype(BF)
    grad_loc[...] = gp[:, :main].astype(BF)

    def scatter(src, dst_of, send, recv):
        @pl.loop(1, n_ep)
        def _(k):
            peer = lax.rem(me + k, n_ep)
            pltpu.make_async_remote_copy(
                src_ref=src.at[pl.ds(peer * slot, slot)],
                dst_ref=dst_of(me * slot),
                send_sem=send,
                recv_sem=recv,
                device_id={"ep": peer},
                device_id_type=MESH,
            ).start()

        pltpu.make_async_copy(src.at[pl.ds(me * slot, slot)], dst_of(me * slot), recv).start()

    part = lax.div(me, n_ep // 2)
    scatter(grad_loc, lambda r: grad_all.at[f, pl.ds(r, slot)], a2a_send.at[1], a2a_recv.at[2])
    scatter(tok_loc, lambda r: tok_all.at[f, pl.ds(r, slot)], a2a_send.at[0], a2a_recv.at[part])

    def swap_relay():
        for h in (0, 1):
            for d, step in ((0, 1), (1, -1)):
                wait_bytes(down_relay.at[h, d], swap_recv.at[2 * h + d])
                for i in (0, 1):
                    put(down_relay.at[h, d, i], down_ring.at[h, 2 * d + i, block(place(2))],
                        swap_send.at[0], swap_recv.at[4 + h], h, step)

    for h in (0, 1):
        for c in range(4):
            down_ring[h, c, :unit] = down[h * unit : (h + 1) * unit, lanes(h, 0, RING[c])]
    swap_relay()

    def gather(buf, send):
        def sem(h, i):
            return ag_recv.at[h * 20 + i]

        def ref(h, fst, snd, q=None):
            o = coord(h, fst, snd)
            first = h * half + (0 if q is None else q * quarter)
            return buf.at[flat(*o), pl.ds(first, half if q is None else quarter)]

        def wait(h, i, fst, snd, q=None):
            wait_bytes(ref(h, fst, snd, q), sem(h, i))

        def send_block(h, i, fst, snd, axis, step, q=None):
            r = ref(h, fst, snd, q)
            put(r, r, send, sem(h, i), axis, step)

        def own(h):
            for i, step in ((0, 1), (1, -1)):
                send_block(h, i, 0, 0, h, step)
            for i, step in ((4, 1), (5, -1)):
                send_block(h, i, 0, 0, 1 - h, step)

        def spread(h, j):
            for i, step in ((0, 1), (1, -1)):
                send_block(h, 4 + 4 * j + i, RING[j], 0, 1 - h, step)

        def s1():
            for i in (0, 1):
                o = (-1, 1)[i]
                for h in (0, 1):
                    wait(h, i, o, 0)
                    send_block(h, 2 + i, o, 0, h, -o, i)
                for h in (0, 1):
                    spread(h, 1 + i)

        def relay(j):
            for i in (0, 1):
                o = (-1, 1)[i]
                for h in (1, 0):
                    wait(h, 4 + 4 * j + i, RING[j], o)
                    send_block(h, 6 + 4 * j + i, RING[j], o, 1 - h, -o, i)

        def s3():
            for h in (0, 1):
                wait(h, 2, 2, 0, 0)
                wait(h, 3, 2, 0, 1)
                spread(h, 3)

        def finish():
            for j in range(4):
                for h in (0, 1):
                    for i in (0, 1):
                        wait(h, 6 + 4 * j + i, RING[j], 2, i)

        return own, s1, relay, s3, finish

    def ring(axis, term, land, n, sem, send):
        q1, q2, fp, fm = 0, n, 2 * n, 4 * n

        def init():
            put(term(2, 0), land(q1, n), send, sem(0), axis, 1)
            put(term(2, 1), land(q2, n), send, sem(1), axis, -1)
            put(term(1, 1), land(fp + n, n), send, sem(2), axis, 1)
            put(term(-1, 0), land(fm, n), send, sem(3), axis, -1)

        def comb():
            for i, k, first, dst in ((0, 1, q1, fp), (1, -1, q2, fm + n)):
                r = land(first, n)
                wait_bytes(r, sem(i))
                r[...] = (r[...].astype(F32) + term(k, i)[...].astype(F32)).astype(BF)
                put(r, land(dst, n), send, sem(4 + i), axis, k)

        def total():
            for first, i in ((fp + n, 2), (fm, 3), (fp, 4), (fm + n, 5)):
                wait_bytes(land(first, n), sem(i))
            return (
                term(0)[...].astype(F32)
                + land(fp, 2 * n)[...].astype(F32)
                + land(fm, 2 * n)[...].astype(F32)
            )

        return init, comb, total

    def reduce(buf, in1, in2, res, send):
        def make(h, j):
            def term(k, q=None):
                o = coord(h, RING[j], k) if j < 4 else coord(h, k, 0)
                first = h * half + (0 if q is None else q * quarter)
                return buf.at[flat(*o), pl.ds(first, half if q is None else quarter)]

            def land(first, n):
                if j < 4:
                    return in1.at[h, j, pl.ds(first, n)]
                return in2.at[h, pl.ds(first, n)]

            def sem(i):
                return rs_recv.at[h * 30 + j * 6 + i]

            init, comb, total = ring(1 - h if j < 4 else h, term, land, quarter, sem, send)

            def fin():
                if j < 4:
                    term(0)[...] = total().astype(BF)
                else:
                    res[pl.ds(h * half, half)] = total().astype(BF)

            return init, comb, fin

        return {(h, j): make(h, j) for h in (0, 1) for j in range(5)}

    def grad_block(axis, o, q=None):
        g = grad_all.at[flat(*coord(axis, o))]
        return g if q is None else g.at[pl.ds(q * half, half)]

    def grad_sem(axis, i):
        return ag_recv.at[40 + axis * 4 + i]

    wait_bytes(grad_all.at[f], a2a_recv.at[2])
    for axis in (0, 1):
        for i, step in ((0, 1), (1, -1)):
            put(grad_block(axis, 0), grad_block(axis, 0), ag_send.at[1], grad_sem(axis, i), axis, step)
    own, s1, relay, s3, finish = gather(tok_all, ag_send.at[0])
    for h in (0, 1):
        wait_bytes(tok_all.at[f, pl.ds(h * half, half)], a2a_recv.at[h])
        own(h)
    for i in (0, 1):
        o = (-1, 1)[i]
        for axis in (0, 1):
            wait_bytes(grad_block(axis, o), grad_sem(axis, i))
            put(grad_block(axis, o, i), grad_block(axis, o, i), ag_send.at[1], grad_sem(axis, 2 + i), axis, -o)
    s1()

    def grad_hidden(h):
        wait_bytes(down_ring.at[h, pl.ds(0, 3)], swap_recv.at[4 + h])
        for i in (0, 1):
            wait_bytes(grad_block(1 - h, 2, i), grad_sem(1 - h, 2 + i))
        term = jnp.zeros((4 * unit, rows), F32)
        for c in range(4):
            term = term + dot(down_ring[h, c], grad_block(1 - h, RING[c])[...], LAST)
        gh_own[pl.ds(h * unit, unit)] = term[:unit]
        gh_send[h] = term[unit:].astype(BF)
        for o in (2, 1, -1):
            put(gh_send.at[h, block(place(o) - 1)], gh_in.at[h, place(-o if o < 2 else 2) - 1],
                small_send.at[2 + h], small_recv.at[2 + h], h, o)

    grad_hidden(0)
    relay(0)
    grad_hidden(1)
    s3()
    relay(1)
    relay(2)
    relay(3)
    n_pair = tok_all.shape[0] // 2
    low = lax.broadcasted_iota(jnp.int32, (half, 128), 1) < 64

    def span(p, size=pair):
        return pl.ds(pl.multiple_of(p * pair, 128), size)

    def rest(p):
        return pl.ds(pl.multiple_of(p * pair + main, 128), 128)

    def tok_pair(p, r=slice(None)):
        return jnp.concatenate(
            [tok_all[2 * p, r, :main], tok_rem[p, r], tok_all[2 * p + 1, r, :main]], axis=1
        )

    def row_at(d):
        return lax.rem(y + d, SIDE)

    def accumulate(p, h):
        r = pl.ds(h * half, half)
        even = tok_all[2 * p, r, main:].astype(F32)
        other = tok_all[2 * p + 1, r, main:].astype(F32)
        tok_rem[p, r] = jnp.where(low, even, other).astype(BF)
        grad_rem[p, r] = pltpu.roll(jnp.where(low, other, even), 64, 1).astype(BF)
        both = jnp.concatenate([gate[span(p)], up[span(p)]], axis=1)
        pre[r] += dot(tok_pair(p, r), both)
        gh_own[:, r] += dot(down[:, rest(p)], grad_rem[p, r], LAST)

    pre[...] = jnp.zeros_like(pre)
    loads[1].wait()
    loads[2].wait()

    @pl.loop(0, 6)
    def _(t):
        accumulate(2 * row_at(3 + lax.div(t, 2)) + lax.rem(t, 2), 0)

    @pl.loop(0, 4)
    def _(t):
        accumulate(2 * t + lax.div(x, 2), 1)

    for h in (0, 1):
        wait_bytes(gh_in.at[h], small_recv.at[2 + h])
        gh_own[pl.ds(h * unit, unit)] += (
            gh_in[h, 0].astype(F32) + gh_in[h, 1].astype(F32) + gh_in[h, 2].astype(F32)
        )
    finish()
    xp = lax.div(x, 2)
    for h in (0, 1):
        @pl.loop(0, (2, 4)[h])
        def _(t, h=h):
            accumulate((2 * row_at(2) + t, 2 * t + 1 - xp)[h], h)

    pg = pre[:, :128]
    pu = pre[:, 128:]
    sg = jax.nn.sigmoid(pg)
    hidden = pg * sg * pu
    hid[...] = hidden.astype(BF)
    turned = jnp.transpose(hidden).astype(BF)
    for h in (0, 1):
        hid_t[h, :unit] = turned[h * unit : (h + 1) * unit]
    for o in (2, 1, -1):
        for h in (0, 1):
            put(hid_t.at[h, block(0)], hid_t.at[h, block(place(-o if o < 2 else 2))],
                small_send.at[h], small_recv.at[h], h, o)
    gh = jnp.transpose(gh_own[...])
    gpre[:, :128] = (gh * pu * sg * (1.0 + pg * (1.0 - sg))).astype(BF)
    gpre[:, 128:] = (gh * (pg * sg)).astype(BF)
    wlow = lax.broadcasted_iota(jnp.int32, (rows, 128), 1) < 64

    def ret_pair(p):
        both = jnp.concatenate([gate[span(p)], up[span(p)]], axis=1)
        r = dot(gpre[...], both, LAST)
        ret_part[2 * p, :, :main] = r[:, :main].astype(BF)
        ret_part[2 * p + 1, :, :main] = r[:, wide:].astype(BF)
        rem = pltpu.roll(r[:, main:wide], 64, 1)
        o = dot(hid[...], down[:, rest(p)])
        ret_part[2 * p, :, main:] = jnp.where(wlow, o, rem).astype(BF)
        ret_part[2 * p + 1, :, main:] = jnp.where(wlow, rem, o).astype(BF)

    rets = reduce(ret_part, ret_in, ret_in2, ret_res, rs_send.at[1])

    def each(step, *order):
        for j in order:
            for h in (0, 1):
                rets[h, j][step]()

    @pl.loop(0, 2)
    def _(t):
        ret_pair(2 * row_at(2) + t)

    rets[1, 3][0]()

    @pl.loop(3, 6)
    def _(t):
        ret_pair(2 * row_at(t) + 1 - xp)

    rets[0, 3][0]()

    @pl.loop(3, 6)
    def _(t):
        ret_pair(2 * row_at(t) + xp)

    each(0, 2, 1, 0)

    outs = []
    for h in (0, 1):
        wait_bytes(hid_t.at[h, pl.ds(0, 3 * unit)], small_recv.at[h])
        hid_g[h] = jnp.transpose(hid_t[h].astype(F32)).astype(BF)
        for c in range(4):
            out_part[h, c] = dot(hid_g[h], down_ring[h, c]).astype(BF)

        def term(k, q=None, h=h):
            r = out_part.at[h, place(k)]
            return r if q is None else r.at[pl.ds(q * half, half)]

        def land(first, n, h=h):
            return out_in.at[h, pl.ds(first, n)]

        outs.append(ring(1 - h, term, land, half, lambda i, h=h: out_recv.at[h * 6 + i], rs_send.at[0]))
        outs[h][0]()
    each(1, 3, 2)

    @pl.loop(0, n_pair)
    def _(p):
        g = dot(tok_pair(p), gpre[...], ROWS).astype(BF)
        ggate[span(p)] = g[:, :128]
        gup[span(p)] = g[:, 128:]
        gdown[:, rest(p)] = dot(hid[...], grad_rem[p], ROWS).astype(BF)

    each(1, 1, 0)
    for h in (0, 1):
        for c in range(4):
            gd_part[h, c] = dot(hid_t[h], grad_block(1 - h, RING[c])[...]).astype(BF)
            gdown[h * unit : (h + 1) * unit, lanes(h, 0, RING[c])] = gd_part[h, c, :unit]
    for h in (0, 1):
        outs[h][1]()
    each(2, 3, 2, 1)
    each(0, 4)
    for i in (0, 1):
        for h in (0, 1):
            for d, step in ((0, 1), (1, -1)):
                put(gd_part.at[h, 2 * d + i, block(place(2))], gd_relay.at[h, d, i],
                    swap_send.at[1], swap_recv.at[6 + 2 * h + d], h, step)
    out_res[...] = (outs[0][2]() + outs[1][2]()).astype(BF)
    scatter(out_res, lambda r: out_back.at[pl.ds(r, slot)], back_send.at[0], back_recv.at[0])
    each(1, 4)
    for c in range(4):
        for h in (0, 1):
            for step in (1, -1):
                put(gd_part.at[h, c, block(place(step))], owned(gdown, h, 0, RING[c]),
                    swap_send.at[1], swap_recv.at[10 + h], h, step)
    each(2, 0)
    each(2, 4)
    scatter(ret_res, lambda r: ret_back.at[pl.ds(r, slot)], back_send.at[1], back_recv.at[1])
    for h in (0, 1):
        for d, step in ((0, 1), (1, -1)):
            wait_bytes(gd_relay.at[h, d], swap_recv.at[6 + 2 * h + d])
            for i in (0, 1):
                put(gd_relay.at[h, d, i], owned(gdown, h, -step, RING[2 * d + i]),
                    swap_send.at[1], swap_recv.at[10 + h], h, step)

    def home(packed, which, hot):
        return dot(dot(pack_ref[which], packed, LAST).astype(BF), hot)

    wait_bytes(out_back, back_recv.at[0])
    hot = hot_ref[...]
    scaled = out_back[...].astype(F32) * w_ref[...]
    high = scaled.astype(BF)
    low_part = (scaled - high.astype(F32)).astype(BF)
    body = pack_ref[0, :, :main]
    partial = dot(dot(body, high, LAST).astype(BF), hot) + dot(dot(body, low_part, LAST).astype(BF), hot)
    wait_bytes(ret_back, back_recv.at[1])
    grad_tok_ref[...] = home(ret_back[...], 1, hot).astype(BF)
    scaled = ret_back[:, main:].astype(F32) * w_ref[...]
    high = scaled.astype(BF)
    low_part = (scaled - high.astype(F32)).astype(BF)
    tail = pack_ref[0, :, main:]
    high = dot(tail, high, LAST).astype(BF)
    low_part = dot(tail, low_part, LAST).astype(BF)
    mixture_ref[...] = (partial + dot(high, hot) + dot(low_part, hot)).astype(BF)

    for h in (0, 1):
        wait_bytes(gd_part.at[h, pl.ds(0, 3)], swap_recv.at[10 + h])
        wait_bytes(hid_t.at[h, pl.ds(0, 3 * unit)], small_send.at[h])
        wait_bytes(gh_send.at[h], small_send.at[2 + h])
    wait_bytes(down_ring, swap_send.at[0])
    wait_bytes(gd_part, swap_send.at[1])
    wait_bytes(tok_loc.at[pl.ds(0, rows - slot)], a2a_send.at[0])
    wait_bytes(grad_loc.at[pl.ds(0, rows - slot)], a2a_send.at[1])
    wait_bytes(tok_all.at[pl.ds(0, 15)], ag_send.at[0])
    wait_bytes(grad_all.at[pl.ds(0, 6)], ag_send.at[1])
    wait_bytes(out_in, rs_send.at[0])
    wait_bytes(ret_part.at[pl.ds(0, 15)], rs_send.at[1])
    wait_bytes(out_res.at[pl.ds(0, rows - slot)], back_send.at[0])
    wait_bytes(ret_res.at[pl.ds(0, rows - slot)], back_send.at[1])


def finish_kernel(*refs):
    n = len(refs) // 2
    stores = [pltpu.make_async_copy(refs[i], refs[n + i], refs[-1].at[i]) for i in range(n)]
    for store in stores:
        store.start()
    for store in stores:
        store.wait()


def per_device(tokens, cotangent, gate_weight, up_weight, down_weight, chosen, counts, gate_prob):
    experts, _, slots = chosen.shape
    n_tok, feats = tokens.shape
    rows = experts * slots
    width = gate_weight.shape[1]
    hidden = gate_weight.shape[2]
    wide, main = 512, 384
    n = width // feats
    vmem = pl.BlockSpec(memory_space=pltpu.VMEM)
    smem = pl.BlockSpec(memory_space=pltpu.SMEM)
    hbm = pl.BlockSpec(memory_space=pl.ANY)
    dma = pltpu.SemaphoreType.DMA
    half = rows // 2
    kept = pl.pallas_call(
        kernel,
        out_shape=(
            pltpu.VMEM((feats, n_tok), BF),
            pltpu.VMEM((feats, n_tok), BF),
            pltpu.VMEM((width, hidden), BF),
            pltpu.VMEM((width, hidden), BF),
            pltpu.VMEM((hidden, width), BF),
        ),
        in_specs=[smem] + [vmem] * 4 + [hbm] * 3,
        out_specs=(vmem,) * 5,
        scratch_shapes=[
            pltpu.VMEM((rows, main), BF),
            pltpu.VMEM((rows, wide), BF),
            pltpu.VMEM((rows, n_tok), BF),
            pltpu.VMEM((rows, 1), F32),
            pltpu.VMEM((2, feats, wide), BF),
            pltpu.VMEM((rows, wide), BF),
            pltpu.VMEM((rows, main), BF),
            pltpu.VMEM((n, rows, wide), BF),
            pltpu.VMEM((n, rows, main), BF),
            pltpu.VMEM((n // 2, rows, 128), BF),
            pltpu.VMEM((n // 2, rows, 128), BF),
            pltpu.VMEM((width, hidden), BF),
            pltpu.VMEM((width, hidden), BF),
            pltpu.VMEM((hidden, width), BF),
            pltpu.VMEM((2, 4, 256, main), BF),
            pltpu.VMEM((2, 2, 2, 64, main), BF),
            pltpu.VMEM((2, 4, 256, main), BF),
            pltpu.VMEM((2, 2, 2, 64, main), BF),
            pltpu.VMEM((rows, hidden), BF),
            pltpu.VMEM((2, 256, rows), BF),
            pltpu.VMEM((2, rows, 256), BF),
            pltpu.VMEM((2, 192, rows), BF),
            pltpu.VMEM((hidden, rows), F32),
            pltpu.VMEM((2, 3, 64, rows), BF),
            pltpu.VMEM((rows, 2 * hidden), F32),
            pltpu.VMEM((rows, 2 * hidden), BF),
            pltpu.VMEM((2, 4, rows, main), BF),
            pltpu.VMEM((n, rows, wide), BF),
            pltpu.VMEM((2, 3 * rows, main), BF),
            pltpu.VMEM((2, 4, 3 * half, wide), BF),
            pltpu.VMEM((2, 3 * half, wide), BF),
            pltpu.VMEM((rows, main), BF),
            pltpu.VMEM((rows, wide), BF),
            dma((3,)),
            dma((2,)),
            dma((3,)),
            dma((2,)),
            dma((48,)),
            dma((2,)),
            dma((60,)),
            dma((12,)),
            dma((2,)),
            dma((2,)),
            dma((2,)),
            dma((12,)),
            dma((4,)),
            dma((4,)),
        ],
        compiler_params=pltpu.CompilerParams(
            collective_id=0, has_side_effects=True, vmem_limit_bytes=52 * 1024 * 1024
        ),
        name="experts",
    )(
        counts[:, 0],
        chosen[:, 0, :],
        gate_prob[:, 0, :],
        tokens.T,
        cotangent.T,
        gate_weight[0],
        up_weight[0],
        down_weight[0],
    )
    mixture, grad_tokens, grad_gate, grad_up, grad_down = pl.pallas_call(
        finish_kernel,
        out_shape=(
            jax.ShapeDtypeStruct((feats, n_tok), BF),
            jax.ShapeDtypeStruct((feats, n_tok), BF),
            jax.ShapeDtypeStruct((width, hidden), BF),
            jax.ShapeDtypeStruct((width, hidden), BF),
            jax.ShapeDtypeStruct((hidden, width), BF),
        ),
        in_specs=[vmem] * 5,
        out_specs=(hbm,) * 5,
        scratch_shapes=[dma((5,))],
        compiler_params=pltpu.CompilerParams(vmem_limit_bytes=16 * 1024 * 1024),
        name="finish",
    )(*kept)
    return mixture.T, grad_tokens.T, grad_gate[None], grad_up[None], grad_down[None]


def solution(mesh):
    placed = (
        P("ep", "fsdp"),
        P("ep", "fsdp"),
        P("ep", None, "fsdp"),
        P("ep", None, "fsdp"),
        P("ep", "fsdp", None),
        P(None, "ep", None),
        P(None, "ep"),
        P(None, "ep", None),
    )
    return jax.shard_map(
        per_device,
        mesh=mesh,
        in_specs=placed,
        out_specs=(
            P("ep", "fsdp"),
            P("ep", "fsdp"),
            P("ep", None, "fsdp"),
            P("ep", None, "fsdp"),
            P("ep", "fsdp", None),
        ),
        check_vma=False,
    )
```

time: 121 us -> 104 us (0.86)
  Pallas kernels: 120 us -> 103 us
    pallas_call x1, Pallas kernels: 116 us -> 100 us  [per_device(): pl.pallas_call(kernel, out_shape=(pltpu.VMEM((feats, n_tok), BF), pltpu.V...]
where the time goes in v3:
time: 104 us
  Pallas kernels  103 us (99%)
    pallas_call x1, Pallas kernels, per_device(): pl.pallas_call(kernel, out_shape=(pltpu.VMEM((feats, n_tok), BF), pltpu.V...  100 us
    pallas_call x1, Pallas kernels, per_device(): pl.pallas_call(finish_kernel, out_shape=(jax.ShapeDtypeStruct((feats, n_t...  2.78 us

profile of v3, /device:TPU:1, one launch (start us, length us, event | category | flops | bytes accessed | tf_op | source)
XLA Modules:
  0.0 103.9 jit_solution(17652729389002907517)
XLA Ops:
  0.6 100.5 %experts.1 = (bf16[448,512]{1,0:T(8,128)(2,1)S(1)}, bf16[448,512]{1,0:T(8,128)(2,1)S(1)}, bf16[7168,128]{1,0:T(8,128)(2,1)S(1)}, bf16[7168,128]{1,0:T(8,128)(2,1)S(1)}, bf16[128,7168]{1,0:T(8,128)(2,1)S(1)}) custom-call(s32[16]{0:T(128)} %bitcast.20, s32[16,16]{1,0:T(8,128)} %bitcast.18, f32[16,16]{1,0:T(8,128)} %bitcast.19, bf16[448,512]{1,0:T(8,128)(2,1)} %bitcast.16, ...), custom_call_target="tpu_custom_call" | custom-call | tf_op jit(solution)/shard_map/experts/pallas_call | solution.py:551
  101.1 2.8 %finish.1 = (bf16[448,512]{1,0:T(8,128)(2,1)}, bf16[448,512]{1,0:T(8,128)(2,1)}, bf16[7168,128]{1,0:T(8,128)(2,1)}, bf16[7168,128]{1,0:T(8,128)(2,1)}, bf16[128,7168]{1,0:T(8,128)(2,1)}) custom-call(bf16[448,512]{1,0:T(8,128)(2,1)S(1)} %get-tuple-element.15.refs_0_, bf16[448,512]{1,0:T(8,128)(2,1)S(1)} %get-tuple-element.16.refs_1_, ...), custom_call_target="tpu_custom_call" | custom-call | tf_op jit(solution)/shard_map/finish/pallas_call | solution.py:625

commit v4 on v3

--- a/solution.py
+++ b/solution.py
@@ -34,9 +34,9 @@
 
 
 def kernel(
-    count_ref, chosen_ref, prob_ref, tok_ref, cot_ref, gate_hbm, up_hbm, down_hbm,
+    count_ref, chosen_ref, prob_ref, tok_hbm, cot_hbm, gate_hbm, up_hbm, down_hbm,
     mixture_ref, grad_tok_ref, ggate, gup, gdown,
-    out_back, ret_back, hot_ref, w_ref, pack_ref,
+    tok_ref, cot_ref, out_back, ret_back, hot_ref, w_ref, pack_ref,
     tok_loc, grad_loc, tok_all, grad_all, tok_rem, grad_rem,
     gate, up, down, down_ring, down_relay, gd_part, gd_relay,
     hid, hid_t, hid_g, gh_send, gh_own, gh_in, pre, gpre,
@@ -54,7 +54,10 @@
     main = grad_all.shape[2]
     rows = tok_all.shape[1]
     half = rows // 2
-    quarter = rows // 4
+    n_seg = 2
+    seg = rows // n_seg
+    piece = seg // 2
+    bit = seg // 4
     feats = tok_ref.shape[0]
     pair = 2 * feats
     slot = 16
@@ -80,10 +83,12 @@
 
     loads = [
         pltpu.make_async_copy(src, dst, w_sem.at[i])
-        for i, (src, dst) in enumerate(((down_hbm, down), (gate_hbm, gate), (up_hbm, up)))
+        for i, (src, dst) in enumerate(
+            ((down_hbm, down), (gate_hbm, gate), (up_hbm, up), (tok_hbm, tok_ref), (cot_hbm, cot_ref))
+        )
     ]
-    for load in loads:
-        load.start()
+    for i in (0, 3, 4, 1, 2):
+        loads[i].start()
 
     def wait_bytes(ref, sem):
         pltpu.make_async_copy(ref, ref, sem).wait()
@@ -104,6 +109,21 @@
 
     def block(i):
         return pl.ds(i * unit, unit)
+
+    loads[0].wait()
+    pl.semaphore_wait(barrier, n_ep + 5)
+
+    for i in (0, 1):
+        for h in (0, 1):
+            for d, step in ((0, 1), (1, -1)):
+                put(owned(down, h, 2, RING[2 * d + i]), down_relay.at[h, d, i],
+                    swap_send.at[0], swap_recv.at[2 * h + d], h, step)
+    for c in range(4):
+        for h in (0, 1):
+            for step in (1, -1):
+                put(owned(down, h, step, RING[c]), down_ring.at[h, c, block(place(-step))],
+                    swap_send.at[0], swap_recv.at[4 + h], h, step)
+
 
     n_tok = tok_ref.shape[1]
     pack_a, pack_b = packings(odd, feats, main, wide)
@@ -125,21 +145,8 @@
     onehot = jnp.where(hit, 1.0, 0.0).astype(BF)
     hot_ref[...] = onehot
 
-    loads[0].wait()
-    pl.semaphore_wait(barrier, n_ep + 5)
-
-    for i in (0, 1):
-        for h in (0, 1):
-            for d, step in ((0, 1), (1, -1)):
-                put(owned(down, h, 2, RING[2 * d + i]), down_relay.at[h, d, i],
-                    swap_send.at[0], swap_recv.at[2 * h + d], h, step)
-    for c in range(4):
-        for h in (0, 1):
-            for step in (1, -1):
-                put(owned(down, h, step, RING[c]), down_ring.at[h, c, block(place(-step))],
-                    swap_send.at[0], swap_recv.at[4 + h], h, step)
-
-
+    loads[3].wait()
+    loads[4].wait()
     tp = dot(dot(onehot, tok_ref[...], LAST).astype(BF), pack_a)
     gp = dot((dot(onehot, cot_ref[...], LAST) * w_ref[...]).astype(BF), pack_b)
     tok_loc[:, :main] = tp[:, :main].astype(BF)
@@ -147,9 +154,10 @@
     grad_loc[...] = gp[:, :main].astype(BF)
 
     def scatter(src, dst_of, send, recv):
-        @pl.loop(1, n_ep)
-        def _(k):
-            peer = lax.rem(me + k, n_ep)
+        @pl.loop(0, n_ep - 1)
+        def _(t):
+            gap = lax.div(t + 1, 2) * (1 - 2 * lax.rem(t, 2))
+            peer = lax.rem(me + n_ep // 2 + gap, n_ep)
             pltpu.make_async_remote_copy(
                 src_ref=src.at[pl.ds(peer * slot, slot)],
                 dst_ref=dst_of(me * slot),
@@ -178,14 +186,14 @@
             down_ring[h, c, :unit] = down[h * unit : (h + 1) * unit, lanes(h, 0, RING[c])]
     swap_relay()
 
-    def gather(buf, send):
+    def gather(buf, send, g):
         def sem(h, i):
-            return ag_recv.at[h * 20 + i]
+            return ag_recv.at[g * 40 + h * 20 + i]
 
         def ref(h, fst, snd, q=None):
             o = coord(h, fst, snd)
-            first = h * half + (0 if q is None else q * quarter)
-            return buf.at[flat(*o), pl.ds(first, half if q is None else quarter)]
+            first = g * seg + h * piece + (0 if q is None else q * bit)
+            return buf.at[flat(*o), pl.ds(first, piece if q is None else bit)]
 
         def wait(h, i, fst, snd, q=None):
             wait_bytes(ref(h, fst, snd, q), sem(h, i))
@@ -261,28 +269,28 @@
 
         return init, comb, total
 
-    def reduce(buf, in1, in2, res, send):
+    def reduce(buf, in1, in2, res, send, g):
         def make(h, j):
             def term(k, q=None):
                 o = coord(h, RING[j], k) if j < 4 else coord(h, k, 0)
-                first = h * half + (0 if q is None else q * quarter)
-                return buf.at[flat(*o), pl.ds(first, half if q is None else quarter)]
+                first = g * seg + h * piece + (0 if q is None else q * bit)
+                return buf.at[flat(*o), pl.ds(first, piece if q is None else bit)]
 
             def land(first, n):
                 if j < 4:
-                    return in1.at[h, j, pl.ds(first, n)]
-                return in2.at[h, pl.ds(first, n)]
+                    return in1.at[g, h, j, pl.ds(first, n)]
+                return in2.at[g, h, pl.ds(first, n)]
 
             def sem(i):
-                return rs_recv.at[h * 30 + j * 6 + i]
-
-            init, comb, total = ring(1 - h if j < 4 else h, term, land, quarter, sem, send)
+                return rs_recv.at[g * 60 + h * 30 + j * 6 + i]
+
+            init, comb, total = ring(1 - h if j < 4 else h, term, land, bit, sem, send)
 
             def fin():
                 if j < 4:
                     term(0)[...] = total().astype(BF)
                 else:
-                    res[pl.ds(h * half, half)] = total().astype(BF)
+                    res[pl.ds(g * seg + h * piece, piece)] = total().astype(BF)
 
             return init, comb, fin
 
@@ -293,22 +301,24 @@
         return g if q is None else g.at[pl.ds(q * half, half)]
 
     def grad_sem(axis, i):
-        return ag_recv.at[40 + axis * 4 + i]
+        return ag_recv.at[n_seg * 40 + axis * 4 + i]
 
     wait_bytes(grad_all.at[f], a2a_recv.at[2])
     for axis in (0, 1):
         for i, step in ((0, 1), (1, -1)):
             put(grad_block(axis, 0), grad_block(axis, 0), ag_send.at[1], grad_sem(axis, i), axis, step)
-    own, s1, relay, s3, finish = gather(tok_all, ag_send.at[0])
-    for h in (0, 1):
-        wait_bytes(tok_all.at[f, pl.ds(h * half, half)], a2a_recv.at[h])
-        own(h)
+    tree = [gather(tok_all, ag_send.at[0], g) for g in range(n_seg)]
+    own, s1, relay, s3, finish = zip(*tree)
+    for g in range(n_seg):
+        wait_bytes(tok_all.at[f, pl.ds(g * seg, seg)], a2a_recv.at[g])
+        for h in (0, 1):
+            own[g](h)
     for i in (0, 1):
         o = (-1, 1)[i]
         for axis in (0, 1):
             wait_bytes(grad_block(axis, o), grad_sem(axis, i))
             put(grad_block(axis, o, i), grad_block(axis, o, i), ag_send.at[1], grad_sem(axis, 2 + i), axis, -o)
-    s1()
+    s1[0]()
 
     def grad_hidden(h):
         wait_bytes(down_ring.at[h, pl.ds(0, 3)], swap_recv.at[4 + h])
@@ -324,14 +334,15 @@
                 small_send.at[2 + h], small_recv.at[2 + h], h, o)
 
     grad_hidden(0)
-    relay(0)
+    relay[0](0)
+    s3[0]()
     grad_hidden(1)
-    s3()
-    relay(1)
-    relay(2)
-    relay(3)
+    relay[0](1)
+    relay[0](2)
+    s1[1]()
+    relay[0](3)
     n_pair = tok_all.shape[0] // 2
-    low = lax.broadcasted_iota(jnp.int32, (half, 128), 1) < 64
+    low = lax.broadcasted_iota(jnp.int32, (seg, 128), 1) < 64
 
     def span(p, size=pair):
         return pl.ds(pl.multiple_of(p * pair, 128), size)
@@ -347,8 +358,8 @@
     def row_at(d):
         return lax.rem(y + d, SIDE)
 
-    def accumulate(p, h):
-        r = pl.ds(h * half, half)
+    def accumulate(p, g):
+        r = pl.ds(g * seg, seg)
         even = tok_all[2 * p, r, main:].astype(F32)
         other = tok_all[2 * p + 1, r, main:].astype(F32)
         tok_rem[p, r] = jnp.where(low, even, other).astype(BF)
@@ -360,78 +371,85 @@
     pre[...] = jnp.zeros_like(pre)
     loads[1].wait()
     loads[2].wait()
-
-    @pl.loop(0, 6)
-    def _(t):
-        accumulate(2 * row_at(3 + lax.div(t, 2)) + lax.rem(t, 2), 0)
-
-    @pl.loop(0, 4)
-    def _(t):
-        accumulate(2 * t + lax.div(x, 2), 1)
-
     for h in (0, 1):
         wait_bytes(gh_in.at[h], small_recv.at[2 + h])
         gh_own[pl.ds(h * unit, unit)] += (
             gh_in[h, 0].astype(F32) + gh_in[h, 1].astype(F32) + gh_in[h, 2].astype(F32)
         )
-    finish()
+    relay[1](0)
+    s3[1]()
+    relay[1](1)
+    relay[1](2)
     xp = lax.div(x, 2)
-    for h in (0, 1):
-        @pl.loop(0, (2, 4)[h])
-        def _(t, h=h):
-            accumulate((2 * row_at(2) + t, 2 * t + 1 - xp)[h], h)
-
-    pg = pre[:, :128]
-    pu = pre[:, 128:]
-    sg = jax.nn.sigmoid(pg)
-    hidden = pg * sg * pu
-    hid[...] = hidden.astype(BF)
-    turned = jnp.transpose(hidden).astype(BF)
+    rets = [reduce(ret_part, ret_in, ret_in2, ret_res, rs_send.at[1], g) for g in range(n_seg)]
+
+    def each(g, step, *order):
+        for j in order:
+            for h in (0, 1):
+                rets[g][h, j][step]()
+
+    def forward(g):
+        finish[g]()
+
+        @pl.loop(0, n_pair)
+        def _(p):
+            accumulate(p, g)
+
+    def turn(g):
+        r = pl.ds(g * seg, seg)
+        pg = pre[r, :128]
+        pu = pre[r, 128:]
+        sg = jax.nn.sigmoid(pg)
+        hid[r] = (pg * sg * pu).astype(BF)
+        gh = jnp.transpose(gh_own[:, g * seg : (g + 1) * seg])
+        gpre[r, :128] = (gh * pu * sg * (1.0 + pg * (1.0 - sg))).astype(BF)
+        gpre[r, 128:] = (gh * (pg * sg)).astype(BF)
+
+    def ret_pair(p, g):
+        r = pl.ds(g * seg, seg)
+        both = jnp.concatenate([gate[span(p)], up[span(p)]], axis=1)
+        t = dot(gpre[r], both, LAST)
+        ret_part[2 * p, r, :main] = t[:, :main].astype(BF)
+        ret_part[2 * p + 1, r, :main] = t[:, wide:].astype(BF)
+        rem = pltpu.roll(t[:, main:wide], 64, 1)
+        o = dot(hid[r], down[:, rest(p)])
+        ret_part[2 * p, r, main:] = jnp.where(low, o, rem).astype(BF)
+        ret_part[2 * p + 1, r, main:] = jnp.where(low, rem, o).astype(BF)
+
+    def back(g):
+        @pl.loop(0, 2)
+        def _(t):
+            ret_pair(2 * row_at(2) + t, g)
+
+        rets[g][1, 3][0]()
+
+        @pl.loop(3, 6)
+        def _(t):
+            ret_pair(2 * row_at(t) + 1 - xp, g)
+
+        rets[g][0, 3][0]()
+
+        @pl.loop(3, 6)
+        def _(t):
+            ret_pair(2 * row_at(t) + xp, g)
+
+        each(g, 0, 2, 1, 0)
+
+    forward(0)
+    relay[1](3)
+    turn(0)
+    back(0)
+    forward(1)
+    turn(1)
+    turned = jnp.transpose(hid[...].astype(F32)).astype(BF)
     for h in (0, 1):
         hid_t[h, :unit] = turned[h * unit : (h + 1) * unit]
     for o in (2, 1, -1):
         for h in (0, 1):
             put(hid_t.at[h, block(0)], hid_t.at[h, block(place(-o if o < 2 else 2))],
                 small_send.at[h], small_recv.at[h], h, o)
-    gh = jnp.transpose(gh_own[...])
-    gpre[:, :128] = (gh * pu * sg * (1.0 + pg * (1.0 - sg))).astype(BF)
-    gpre[:, 128:] = (gh * (pg * sg)).astype(BF)
-    wlow = lax.broadcasted_iota(jnp.int32, (rows, 128), 1) < 64
-
-    def ret_pair(p):
-        both = jnp.concatenate([gate[span(p)], up[span(p)]], axis=1)
-        r = dot(gpre[...], both, LAST)
-        ret_part[2 * p, :, :main] = r[:, :main].astype(BF)
-        ret_part[2 * p + 1, :, :main] = r[:, wide:].astype(BF)
-        rem = pltpu.roll(r[:, main:wide], 64, 1)
-        o = dot(hid[...], down[:, rest(p)])
-        ret_part[2 * p, :, main:] = jnp.where(wlow, o, rem).astype(BF)
-        ret_part[2 * p + 1, :, main:] = jnp.where(wlow, rem, o).astype(BF)
-
-    rets = reduce(ret_part, ret_in, ret_in2, ret_res, rs_send.at[1])
-
-    def each(step, *order):
-        for j in order:
-            for h in (0, 1):
-                rets[h, j][step]()
-
-    @pl.loop(0, 2)
-    def _(t):
-        ret_pair(2 * row_at(2) + t)
-
-    rets[1, 3][0]()
-
-    @pl.loop(3, 6)
-    def _(t):
-        ret_pair(2 * row_at(t) + 1 - xp)
-
-    rets[0, 3][0]()
-
-    @pl.loop(3, 6)
-    def _(t):
-        ret_pair(2 * row_at(t) + xp)
-
-    each(0, 2, 1, 0)
+    back(1)
+    each(0, 1, 3, 2)
 
     outs = []
     for h in (0, 1):
@@ -449,7 +467,17 @@
 
         outs.append(ring(1 - h, term, land, half, lambda i, h=h: out_recv.at[h * 6 + i], rs_send.at[0]))
         outs[h][0]()
-    each(1, 3, 2)
+    each(0, 1, 1, 0)
+    for h in (0, 1):
+        outs[h][1]()
+    each(1, 1, 3, 2)
+    for h in (0, 1):
+        for c in range(4):
+            gd_part[h, c] = dot(hid_t[h], grad_block(1 - h, RING[c])[...]).astype(BF)
+            gdown[h * unit : (h + 1) * unit, lanes(h, 0, RING[c])] = gd_part[h, c, :unit]
+    each(0, 2, 3, 2, 1)
+    each(0, 0, 4)
+    each(1, 1, 1, 0)
 
     @pl.loop(0, n_pair)
     def _(p):
@@ -458,31 +486,50 @@
         gup[span(p)] = g[:, 128:]
         gdown[:, rest(p)] = dot(hid[...], grad_rem[p], ROWS).astype(BF)
 
-    each(1, 1, 0)
-    for h in (0, 1):
-        for c in range(4):
-            gd_part[h, c] = dot(hid_t[h], grad_block(1 - h, RING[c])[...]).astype(BF)
-            gdown[h * unit : (h + 1) * unit, lanes(h, 0, RING[c])] = gd_part[h, c, :unit]
-    for h in (0, 1):
-        outs[h][1]()
-    each(2, 3, 2, 1)
-    each(0, 4)
+    out_res[...] = (outs[0][2]() + outs[1][2]()).astype(BF)
+    scatter(out_res, lambda r: out_back.at[pl.ds(r, slot)], back_send.at[0], back_recv.at[0])
+    each(0, 1, 4)
+    each(1, 2, 3, 2, 1)
+    each(1, 0, 4)
     for i in (0, 1):
         for h in (0, 1):
             for d, step in ((0, 1), (1, -1)):
                 put(gd_part.at[h, 2 * d + i, block(place(2))], gd_relay.at[h, d, i],
                     swap_send.at[1], swap_recv.at[6 + 2 * h + d], h, step)
-    out_res[...] = (outs[0][2]() + outs[1][2]()).astype(BF)
-    scatter(out_res, lambda r: out_back.at[pl.ds(r, slot)], back_send.at[0], back_recv.at[0])
-    each(1, 4)
+
+    def ret_home(g):
+        each(g, 2, 0)
+        each(g, 2, 4)
+        n_part = n_ep // n_seg
+        there = ret_back.at[pl.ds(me * slot, slot)]
+
+        @pl.loop(0, n_part)
+        def _(t):
+            peer = g * n_part + lax.rem(me + n_part // 2 + t, n_part)
+
+            @pl.when(peer != me)
+            def _():
+                pltpu.make_async_remote_copy(
+                    src_ref=ret_res.at[pl.ds(peer * slot, slot)],
+                    dst_ref=there,
+                    send_sem=back_send.at[1],
+                    recv_sem=back_recv.at[1],
+                    device_id={"ep": peer},
+                    device_id_type=MESH,
+                ).start()
+
+            @pl.when(peer == me)
+            def _():
+                pltpu.make_async_copy(ret_res.at[pl.ds(me * slot, slot)], there, back_recv.at[1]).start()
+
+    ret_home(0)
+    each(1, 1, 4)
     for c in range(4):
         for h in (0, 1):
             for step in (1, -1):
                 put(gd_part.at[h, c, block(place(step))], owned(gdown, h, 0, RING[c]),
                     swap_send.at[1], swap_recv.at[10 + h], h, step)
-    each(2, 0)
-    each(2, 4)
-    scatter(ret_res, lambda r: ret_back.at[pl.ds(r, slot)], back_send.at[1], back_recv.at[1])
+    ret_home(1)
     for h in (0, 1):
         for d, step in ((0, 1), (1, -1)):
             wait_bytes(gd_relay.at[h, d], swap_recv.at[6 + 2 * h + d])
@@ -557,9 +604,11 @@
             pltpu.VMEM((width, hidden), BF),
             pltpu.VMEM((hidden, width), BF),
         ),
-        in_specs=[smem] + [vmem] * 4 + [hbm] * 3,
+        in_specs=[smem] + [vmem] * 2 + [hbm] * 5,
         out_specs=(vmem,) * 5,
         scratch_shapes=[
+            pltpu.VMEM((feats, n_tok), BF),
+            pltpu.VMEM((feats, n_tok), BF),
             pltpu.VMEM((rows, main), BF),
             pltpu.VMEM((rows, wide), BF),
             pltpu.VMEM((rows, n_tok), BF),
@@ -589,17 +638,17 @@
             pltpu.VMEM((2, 4, rows, main), BF),
             pltpu.VMEM((n, rows, wide), BF),
             pltpu.VMEM((2, 3 * rows, main), BF),
-            pltpu.VMEM((2, 4, 3 * half, wide), BF),
-            pltpu.VMEM((2, 3 * half, wide), BF),
+            pltpu.VMEM((2, 2, 4, 3 * half // 2, wide), BF),
+            pltpu.VMEM((2, 2, 3 * half // 2, wide), BF),
             pltpu.VMEM((rows, main), BF),
             pltpu.VMEM((rows, wide), BF),
-            dma((3,)),
+            dma((5,)),
             dma((2,)),
             dma((3,)),
             dma((2,)),
-            dma((48,)),
+            dma((88,)),
             dma((2,)),
-            dma((60,)),
+            dma((120,)),
             dma((12,)),
             dma((2,)),
             dma((2,)),

time: 104 us -> 96.9 us (0.932)
  Pallas kernels: 103 us -> 95.6 us
    pallas_call x1, Pallas kernels: 100 us -> 92.8 us  [per_device(): pl.pallas_call(kernel, out_shape=(pltpu.VMEM((feats, n_tok), BF), pltpu.V...]
where the time goes in v4:
time: 96.9 us; the launch traced here: 96.2 us
  Pallas kernels  95.6 us (99%)
    pallas_call x1, Pallas kernels, per_device(): pl.pallas_call(kernel, out_shape=(pltpu.VMEM((feats, n_tok), BF), pltpu.V...  92.8 us
    pallas_call x1, Pallas kernels, per_device(): pl.pallas_call(finish_kernel, out_shape=(jax.ShapeDtypeStruct((feats, n_t...  2.78 us

profile of v4, /device:TPU:1, one launch (start us, length us, event | category | flops | bytes accessed | tf_op | source)
XLA Modules:
  0.0 96.2 jit_solution(7333337691829136790)
XLA Ops:
  0.6 92.8 %experts.1 = (bf16[448,512]{1,0:T(8,128)(2,1)S(1)}, bf16[448,512]{1,0:T(8,128)(2,1)S(1)}, bf16[7168,128]{1,0:T(8,128)(2,1)S(1)}, bf16[7168,128]{1,0:T(8,128)(2,1)S(1)}, bf16[128,7168]{1,0:T(8,128)(2,1)S(1)}) custom-call(s32[16]{0:T(128)} %bitcast.20, s32[16,16]{1,0:T(8,128)} %bitcast.18, f32[16,16]{1,0:T(8,128)} %bitcast.19, bf16[448,512]{1,0:T(8,128)(2,1)} %bitcast.16, ...), custom_call_target="tpu_custom_call" | custom-call | tf_op jit(solution)/shard_map/experts/pallas_call | solution.py:598
  93.4 2.8 %finish.1 = (bf16[448,512]{1,0:T(8,128)(2,1)}, bf16[448,512]{1,0:T(8,128)(2,1)}, bf16[7168,128]{1,0:T(8,128)(2,1)}, bf16[7168,128]{1,0:T(8,128)(2,1)}, bf16[128,7168]{1,0:T(8,128)(2,1)}) custom-call(bf16[448,512]{1,0:T(8,128)(2,1)S(1)} %get-tuple-element.15.refs_0_, bf16[448,512]{1,0:T(8,128)(2,1)S(1)} %get-tuple-element.16.refs_1_, ...), custom_call_target="tpu_custom_call" | custom-call | tf_op jit(solution)/shard_map/finish/pallas_call | solution.py:674

commit v5 on v4

--- a/solution.py
+++ b/solution.py
@@ -18,25 +18,10 @@
     return lax.dot_general(a, b, dims, preferred_element_type=F32)
 
 
-def packings(odd, feats, main, wide):
-    fi = lax.broadcasted_iota(jnp.int32, (feats, main), 0)
-    fj = lax.broadcasted_iota(jnp.int32, (feats, main), 1)
-    body = jnp.where(fi - fj == 64 * odd, 1.0, 0.0)
-    ti = lax.broadcasted_iota(jnp.int32, (feats, wide - main), 0)
-    tj = lax.broadcasted_iota(jnp.int32, (feats, wide - main), 1)
-    where = jnp.where(odd == 1, ti, ti - main)
-
-    def packing(low):
-        tail = jnp.where((tj - where == low) & (tj >= low) & (tj < low + 64), 1.0, 0.0)
-        return jnp.concatenate([body, tail], axis=1).astype(BF)
-
-    return packing(64 * odd), packing(64 - 64 * odd)
-
-
 def kernel(
     count_ref, chosen_ref, prob_ref, tok_hbm, cot_hbm, gate_hbm, up_hbm, down_hbm,
     mixture_ref, grad_tok_ref, ggate, gup, gdown,
-    tok_ref, cot_ref, out_back, ret_back, hot_ref, w_ref, pack_ref,
+    tok_ref, cot_ref, out_back, ret_back, hot_ref, w_ref, mix_t,
     tok_loc, grad_loc, tok_all, grad_all, tok_rem, grad_rem,
     gate, up, down, down_ring, down_relay, gd_part, gd_relay,
     hid, hid_t, hid_g, gh_send, gh_own, gh_in, pre, gpre,
@@ -58,7 +43,7 @@
     seg = rows // n_seg
     piece = seg // 2
     bit = seg // 4
-    feats = tok_ref.shape[0]
+    feats = tok_hbm.shape[0]
     pair = 2 * feats
     slot = 16
     unit = 64
@@ -84,7 +69,8 @@
     loads = [
         pltpu.make_async_copy(src, dst, w_sem.at[i])
         for i, (src, dst) in enumerate(
-            ((down_hbm, down), (gate_hbm, gate), (up_hbm, up), (tok_hbm, tok_ref), (cot_hbm, cot_ref))
+            ((down_hbm, down), (gate_hbm, gate), (up_hbm, up), (tok_hbm, tok_ref.at[pl.ds(0, tok_hbm.shape[0])]),
+             (cot_hbm, cot_ref.at[pl.ds(0, tok_hbm.shape[0])]))
         )
     ]
     for i in (0, 3, 4, 1, 2):
@@ -126,9 +112,8 @@
 
 
     n_tok = tok_ref.shape[1]
-    pack_a, pack_b = packings(odd, feats, main, wide)
-    pack_ref[0] = pack_a
-    pack_ref[1] = pack_b
+    tok_ref[feats:] = jnp.zeros((wide - feats, n_tok), BF)
+    cot_ref[feats:] = jnp.zeros((wide - feats, n_tok), BF)
     j = lax.broadcasted_iota(jnp.int32, (1, slot), 1)
     index, weight = [], []
     for e in range(n_ep):
@@ -147,19 +132,20 @@
 
     loads[3].wait()
     loads[4].wait()
-    tp = dot(dot(onehot, tok_ref[...], LAST).astype(BF), pack_a)
-    gp = dot((dot(onehot, cot_ref[...], LAST) * w_ref[...]).astype(BF), pack_b)
+    turn_by = lax.rem(wide - 64 * odd, wide)
+    gp = pltpu.roll(dot(onehot, cot_ref[...], LAST) * w_ref[...], turn_by, 1)
+    tp = pltpu.roll(dot(onehot, tok_ref[...], LAST), turn_by, 1)
     tok_loc[:, :main] = tp[:, :main].astype(BF)
-    tok_loc[:, main:] = (tp[:, main:] + gp[:, main:]).astype(BF)
+    tok_loc[:, main:] = (tp[:, main:] + pltpu.roll(gp[:, main:], 64, 1)).astype(BF)
     grad_loc[...] = gp[:, :main].astype(BF)
 
-    def scatter(src, dst_of, send, recv):
+    def scatter(src, dst_of, send, recv, cols=slice(None)):
         @pl.loop(0, n_ep - 1)
         def _(t):
             gap = lax.div(t + 1, 2) * (1 - 2 * lax.rem(t, 2))
             peer = lax.rem(me + n_ep // 2 + gap, n_ep)
             pltpu.make_async_remote_copy(
-                src_ref=src.at[pl.ds(peer * slot, slot)],
+                src_ref=src.at[pl.ds(peer * slot, slot), cols],
                 dst_ref=dst_of(me * slot),
                 send_sem=send,
                 recv_sem=recv,
@@ -167,11 +153,16 @@
                 device_id_type=MESH,
             ).start()
 
-        pltpu.make_async_copy(src.at[pl.ds(me * slot, slot)], dst_of(me * slot), recv).start()
+        pltpu.make_async_copy(src.at[pl.ds(me * slot, slot), cols], dst_of(me * slot), recv).start()
 
     part = lax.div(me, n_ep // 2)
-    scatter(grad_loc, lambda r: grad_all.at[f, pl.ds(r, slot)], a2a_send.at[1], a2a_recv.at[2])
-    scatter(tok_loc, lambda r: tok_all.at[f, pl.ds(r, slot)], a2a_send.at[0], a2a_recv.at[part])
+    def lane_half(i):
+        return pl.ds(i * (wide // 2), wide // 2)
+
+    for i in (0, 1):
+        scatter(tok_loc, lambda r: tok_all.at[f, pl.ds(r, slot), lane_half(i)], a2a_send.at[0],
+                a2a_recv.at[2 * part + i], lane_half(i))
+    scatter(grad_loc, lambda r: grad_all.at[f, pl.ds(r, slot)], a2a_send.at[1], a2a_recv.at[4])
 
     def swap_relay():
         for h in (0, 1):
@@ -202,11 +193,12 @@
             r = ref(h, fst, snd, q)
             put(r, r, send, sem(h, i), axis, step)
 
-        def own(h):
+        def own(h, cols):
+            r = ref(h, 0, 0).at[:, cols]
             for i, step in ((0, 1), (1, -1)):
-                send_block(h, i, 0, 0, h, step)
+                put(r, r, send, sem(h, i), h, step)
             for i, step in ((4, 1), (5, -1)):
-                send_block(h, i, 0, 0, 1 - h, step)
+                put(r, r, send, sem(h, i), 1 - h, step)
 
         def spread(h, j):
             for i, step in ((0, 1), (1, -1)):
@@ -303,22 +295,18 @@
     def grad_sem(axis, i):
         return ag_recv.at[n_seg * 40 + axis * 4 + i]
 
-    wait_bytes(grad_all.at[f], a2a_recv.at[2])
+    tree = [gather(tok_all, ag_send.at[0], g) for g in range(n_seg)]
+    own, s1, relay, s3, finish = zip(*tree)
+    for i in (0, 1):
+        for g in range(n_seg):
+            wait_bytes(tok_all.at[f, pl.ds(g * seg, seg), lane_half(i)], a2a_recv.at[2 * g + i])
+            for h in (0, 1):
+                own[g](h, lane_half(i))
+    s1[0]()
+    wait_bytes(grad_all.at[f], a2a_recv.at[4])
     for axis in (0, 1):
         for i, step in ((0, 1), (1, -1)):
             put(grad_block(axis, 0), grad_block(axis, 0), ag_send.at[1], grad_sem(axis, i), axis, step)
-    tree = [gather(tok_all, ag_send.at[0], g) for g in range(n_seg)]
-    own, s1, relay, s3, finish = zip(*tree)
-    for g in range(n_seg):
-        wait_bytes(tok_all.at[f, pl.ds(g * seg, seg)], a2a_recv.at[g])
-        for h in (0, 1):
-            own[g](h)
-    for i in (0, 1):
-        o = (-1, 1)[i]
-        for axis in (0, 1):
-            wait_bytes(grad_block(axis, o), grad_sem(axis, i))
-            put(grad_block(axis, o, i), grad_block(axis, o, i), ag_send.at[1], grad_sem(axis, 2 + i), axis, -o)
-    s1[0]()
 
     def grad_hidden(h):
         wait_bytes(down_ring.at[h, pl.ds(0, 3)], swap_recv.at[4 + h])
@@ -333,13 +321,17 @@
             put(gh_send.at[h, block(place(o) - 1)], gh_in.at[h, place(-o if o < 2 else 2) - 1],
                 small_send.at[2 + h], small_recv.at[2 + h], h, o)
 
-    grad_hidden(0)
     relay[0](0)
     s3[0]()
-    grad_hidden(1)
+    for i in (0, 1):
+        o = (-1, 1)[i]
+        for axis in (0, 1):
+            wait_bytes(grad_block(axis, o), grad_sem(axis, i))
+            put(grad_block(axis, o, i), grad_block(axis, o, i), ag_send.at[1], grad_sem(axis, 2 + i), axis, -o)
     relay[0](1)
     relay[0](2)
     s1[1]()
+    grad_hidden(0)
     relay[0](3)
     n_pair = tok_all.shape[0] // 2
     low = lax.broadcasted_iota(jnp.int32, (seg, 128), 1) < 64
@@ -371,12 +363,8 @@
     pre[...] = jnp.zeros_like(pre)
     loads[1].wait()
     loads[2].wait()
-    for h in (0, 1):
-        wait_bytes(gh_in.at[h], small_recv.at[2 + h])
-        gh_own[pl.ds(h * unit, unit)] += (
-            gh_in[h, 0].astype(F32) + gh_in[h, 1].astype(F32) + gh_in[h, 2].astype(F32)
-        )
     relay[1](0)
+    grad_hidden(1)
     s3[1]()
     relay[1](1)
     relay[1](2)
@@ -437,6 +425,11 @@
 
     forward(0)
     relay[1](3)
+    for h in (0, 1):
+        wait_bytes(gh_in.at[h], small_recv.at[2 + h])
+        gh_own[pl.ds(h * unit, unit)] += (
+            gh_in[h, 0].astype(F32) + gh_in[h, 1].astype(F32) + gh_in[h, 2].astype(F32)
+        )
     turn(0)
     back(0)
     forward(1)
@@ -537,25 +530,26 @@
                 put(gd_relay.at[h, d, i], owned(gdown, h, -step, RING[2 * d + i]),
                     swap_send.at[1], swap_recv.at[10 + h], h, step)
 
-    def home(packed, which, hot):
-        return dot(dot(pack_ref[which], packed, LAST).astype(BF), hot)
+    hot = hot_ref[...]
+    body_at = pl.ds(pl.multiple_of(64 * odd, 64), main)
+    rest_at = pl.ds(pl.multiple_of(main * (1 - odd), 64), 64)
+
+    def exact(t):
+        high = t.astype(BF)
+        return dot(high, hot) + dot((t - high.astype(F32)).astype(BF), hot)
 
     wait_bytes(out_back, back_recv.at[0])
-    hot = hot_ref[...]
-    scaled = out_back[...].astype(F32) * w_ref[...]
-    high = scaled.astype(BF)
-    low_part = (scaled - high.astype(F32)).astype(BF)
-    body = pack_ref[0, :, :main]
-    partial = dot(dot(body, high, LAST).astype(BF), hot) + dot(dot(body, low_part, LAST).astype(BF), hot)
+    scaled = jnp.transpose(out_back[...].astype(F32) * w_ref[...])
+    mixture_ref[body_at] = exact(scaled).astype(BF)
     wait_bytes(ret_back, back_recv.at[1])
-    grad_tok_ref[...] = home(ret_back[...], 1, hot).astype(BF)
-    scaled = ret_back[:, main:].astype(F32) * w_ref[...]
-    high = scaled.astype(BF)
-    low_part = (scaled - high.astype(F32)).astype(BF)
-    tail = pack_ref[0, :, main:]
-    high = dot(tail, high, LAST).astype(BF)
-    low_part = dot(tail, low_part, LAST).astype(BF)
-    mixture_ref[...] = (partial + dot(high, hot) + dot(low_part, hot)).astype(BF)
+    tail = ret_back[:, main:].astype(F32)
+    mix_t[0] = jnp.transpose(tail * w_ref[...])
+    mix_t[1] = jnp.transpose(tail)
+    back_t = jnp.transpose(ret_back[:, :main].astype(F32)).astype(BF)
+    grad_tok_ref[body_at] = dot(back_t, hot).astype(BF)
+    mixture_ref[rest_at] = exact(mix_t[0, pl.ds(pl.multiple_of(64 * odd, 64), 64)]).astype(BF)
+    piece_t = mix_t[1, pl.ds(pl.multiple_of(64 - 64 * odd, 64), 64)].astype(BF)
+    grad_tok_ref[rest_at] = dot(piece_t, hot).astype(BF)
 
     for h in (0, 1):
         wait_bytes(gd_part.at[h, pl.ds(0, 3)], swap_recv.at[10 + h])
@@ -607,13 +601,13 @@
         in_specs=[smem] + [vmem] * 2 + [hbm] * 5,
         out_specs=(vmem,) * 5,
         scratch_shapes=[
-            pltpu.VMEM((feats, n_tok), BF),
-            pltpu.VMEM((feats, n_tok), BF),
+            pltpu.VMEM((wide, n_tok), BF),
+            pltpu.VMEM((wide, n_tok), BF),
             pltpu.VMEM((rows, main), BF),
             pltpu.VMEM((rows, wide), BF),
             pltpu.VMEM((rows, n_tok), BF),
             pltpu.VMEM((rows, 1), F32),
-            pltpu.VMEM((2, feats, wide), BF),
+            pltpu.VMEM((2, wide - main, rows), F32),
             pltpu.VMEM((rows, wide), BF),
             pltpu.VMEM((rows, main), BF),
             pltpu.VMEM((n, rows, wide), BF),
@@ -644,7 +638,7 @@
             pltpu.VMEM((rows, wide), BF),
             dma((5,)),
             dma((2,)),
-            dma((3,)),
+            dma((5,)),
             dma((2,)),
             dma((88,)),
             dma((2,)),

time: 96.9 us -> 95.8 us (0.989)
  Pallas kernels: 95.6 us -> 93.9 us
    pallas_call x1, Pallas kernels: 92.8 us -> 91.1 us  [per_device(): pl.pallas_call(kernel, out_shape=(pltpu.VMEM((feats, n_tok), BF), pltpu.V...]
where the time goes in v5:
time: 95.8 us; the launch traced here: 94.6 us
  Pallas kernels  93.9 us (98%)
    pallas_call x1, Pallas kernels, per_device(): pl.pallas_call(kernel, out_shape=(pltpu.VMEM((feats, n_tok), BF), pltpu.V...  91.1 us
    pallas_call x1, Pallas kernels, per_device(): pl.pallas_call(finish_kernel, out_shape=(jax.ShapeDtypeStruct((feats, n_t...  2.78 us

profile of v5, /device:TPU:1, one launch (start us, length us, event | category | flops | bytes accessed | tf_op | source)
XLA Modules:
  0.0 94.6 jit_solution(15846426419432183187)
XLA Ops:
  0.6 91.1 %experts.1 = (bf16[448,512]{1,0:T(8,128)(2,1)S(1)}, bf16[448,512]{1,0:T(8,128)(2,1)S(1)}, bf16[7168,128]{1,0:T(8,128)(2,1)S(1)}, bf16[7168,128]{1,0:T(8,128)(2,1)S(1)}, bf16[128,7168]{1,0:T(8,128)(2,1)S(1)}) custom-call(s32[16]{0:T(128)} %bitcast.20, s32[16,16]{1,0:T(8,128)} %bitcast.18, f32[16,16]{1,0:T(8,128)} %bitcast.19, bf16[448,512]{1,0:T(8,128)(2,1)} %bitcast.16, ...), custom_call_target="tpu_custom_call" | custom-call | tf_op jit(solution)/shard_map/experts/pallas_call | solution.py:592
  91.8 2.8 %finish.1 = (bf16[448,512]{1,0:T(8,128)(2,1)}, bf16[448,512]{1,0:T(8,128)(2,1)}, bf16[7168,128]{1,0:T(8,128)(2,1)}, bf16[7168,128]{1,0:T(8,128)(2,1)}, bf16[128,7168]{1,0:T(8,128)(2,1)}) custom-call(bf16[448,512]{1,0:T(8,128)(2,1)S(1)} %get-tuple-element.15.refs_0_, bf16[448,512]{1,0:T(8,128)(2,1)S(1)} %get-tuple-element.16.refs_1_, ...), custom_call_target="tpu_custom_call" | custom-call | tf_op jit(solution)/shard_map/finish/pallas_call | solution.py:668
